TPU v7x, 256 devices: a whole 4x4x8 slice. The times are simulated.
256 devices in a mesh: seq: 32 (over z, y), head: 8 (over x, core).
Axes of the slice: x: 4, y: 4, z: 8, core: 2. Of those that a mesh axis runs over, the one named last changes fastest.
Arguments:
- x_in: bfloat16 [4096, 8192], P('seq', 'head'), may hold values from -6 to 6
- z_gate: bfloat16 [4096, 8192], P('seq', 'head'), may hold values from -6 to 6
- b_in: bfloat16 [4096, 2048], P('seq', 'head'), may hold values from -0.75 to 0.75
- c_in: bfloat16 [4096, 2048], P('seq', 'head'), may hold values from -0.75 to 0.75
- log_decay: float32 [4096, 128], P('seq', 'head'), may hold values from 0 to 1.5
- step_size: float32 [4096, 128], P('seq', 'head'), may hold values from 0.3 to 3
- d_skip: float32 [128], P('head'), may hold values from 0.5 to 2
- norm_gain: float32 [8192], P('head'), may hold values from 0.25 to 1.75
- w_out: bfloat16 [8192, 4096], P('head'), may hold values from -0.0625 to 0.0625
- residual: bfloat16 [4096, 4096], P(('seq', 'head')), may hold values from -8 to 8
- final_gain: float32 [4096], replicated, may hold values from 0.25 to 1.75
- vocab: bfloat16 [65536, 4096], P(('seq', 'head')), may hold values from -12 to 12
- targets: int32 [32, 128], P(None, 'head'), may hold values from 0 to 65535
Outputs:
- hidden_out: float32 [4096, 4096], P(('seq', 'head'))
- logprob: float32 [4096], P(('seq', 'head'))
All inputs are finite; a program needn't handle non-finite values.
Results may differ from a plain program's by a relative error of at most 0.0029.
Values may be sent and summed in bfloat16 or wider, within the bound.
No kernel may reach another device: no remote copies, remote signals or barrier semaphores. Data moves between devices by JAX's collectives and lax.ppermute only.
A program may use at most 128 MiB of HBM per device.

v0:
```python
import jax
import jax.numpy as jnp
from jax import lax
from jax.sharding import PartitionSpec as P

SCAN_LANE_NUMBER = 128
HEAD_DIM = 64
STATE = 256
GROUPS = 8
INNER = 8192


epsilon = 1e-05
highest = lax.Precision.HIGHEST


def carried_in(value, axis, combine, identity):
    count, mine = (lax.axis_size(axis), lax.axis_index(axis))
    everything = jax.tree.map(lambda part: lax.all_gather(part, axis), value)
    start = jax.tree.map(
        lambda part, zero: jnp.broadcast_to(jnp.asarray(zero, part.dtype), part.shape),
        value,
        identity,
    )

    def hop(k, before):
        reached = k < mine
        new = combine(before, jax.tree.map(lambda part: part[k], everything))
        return jax.tree.map(lambda a, b: jnp.where(reached, a, b), new, before)

    return lax.fori_loop(0, count, hop, start)


def joined(part, axis, combine):
    gathered = jax.tree.map(lambda a: lax.all_gather(a, axis), part)

    def take(source):
        return jax.tree.map(lambda a: lax.dynamic_index_in_dim(a, source, 0, False), gathered)

    return lax.fori_loop(
        1, lax.axis_size(axis), lambda source, state: combine(state, take(source)), take(0)
    )


def local_terms(inputs, b_rows, c_rows, decays, step_rows, per_group):
    length = inputs.shape[0]
    cumulative = jnp.cumsum(decays, axis=0)
    by_head = cumulative.T
    gaps = by_head[:, None, :] - by_head[:, :, None]
    positions = jnp.arange(length)
    causal = positions[None, :] <= positions[:, None]
    segment_w = jnp.where(causal[None], jnp.exp(jnp.minimum(gaps, 0.0)), 0.0)
    scores = jnp.einsum("tgn,sgn->gts", c_rows, b_rows, precision=highest)
    head_scores = jnp.repeat(scores, per_group, axis=0)
    weights = segment_w * head_scores * step_rows.T[:, None, :]
    within = jnp.einsum("hts,shp->thp", weights, inputs, precision=highest)
    last = cumulative[-1]
    end_weight = jnp.exp(last[None, :] - cumulative) * step_rows
    b_heads = jnp.repeat(b_rows, per_group, axis=1)
    end_state = jnp.einsum(
        "shp,shn->hpn", inputs * end_weight[:, :, None], b_heads, precision=highest
    )
    return (within, cumulative, end_state, jnp.exp(-last))


def carried(c_rows, cumulative, state, per_group):
    c_heads = jnp.repeat(c_rows, per_group, axis=1)
    return jnp.exp(-cumulative)[:, :, None] * jnp.einsum(
        "thn,hpn->thp", c_heads, state, precision=highest
    )


def chain(earlier, later):
    return (earlier[0] * later[0], later[0][:, None, None] * earlier[1] + later[1])


def vocab_fold(token_all, wanted, offset):

    def update(carry, piece, start):
        top, total, picked = carry
        logits = lax.dot_general(
            token_all, piece, (((1,), (1,)), ((), ())), preferred_element_type=jnp.float32
        )
        new_top = jnp.max(logits, axis=1)
        total = total * jnp.exp(top - new_top) + jnp.sum(jnp.exp(logits - new_top[:, None]), axis=1)
        vocab_ids = offset + lax.broadcasted_iota(jnp.int32, (1, piece.shape[0]), 1)
        picked = jnp.sum(jnp.where(vocab_ids == wanted[:, None], logits, 0.0), axis=1)
        return (new_top, total, picked)

    return update


def combine(first, second):
    top = jnp.maximum(first[0], second[0])
    total = first[1] * jnp.exp(first[0] - top) + second[1] * jnp.exp(second[0] - top)
    return (top, total, first[2] + second[2])


def start_triple(count):
    return (
        jnp.full((count,), -jnp.inf, jnp.float32),
        jnp.zeros((count,), jnp.float32),
        jnp.zeros((count,), jnp.float32),
    )


def shards(
    x_in,
    z_gate,
    b_in,
    c_in,
    log_decay,
    step_size,
    d_skip,
    norm_gain,
    w_out,
    residual,
    final_gain,
    vocab,
    targets,
):
    per_group = SCAN_LANE_NUMBER // GROUPS
    length = x_in.shape[0]
    head_count = log_decay.shape[1]
    group_count = b_in.shape[1] // STATE
    inputs = x_in.astype(jnp.float32).reshape(length, head_count, HEAD_DIM)
    b_rows = b_in.astype(jnp.float32).reshape(length, group_count, STATE)
    c_rows = c_in.astype(jnp.float32).reshape(length, group_count, STATE)
    within, cumulative, end_state, decay = local_terms(
        inputs, b_rows, c_rows, log_decay, step_size, per_group
    )
    identity = (jnp.ones_like(decay), jnp.zeros_like(end_state))
    incoming = carried_in((decay, end_state), "seq", chain, identity)
    mixed = (
        within
        + carried(c_rows, cumulative, incoming[1], per_group)
        + d_skip[None, :, None] * inputs
    )
    gated = mixed.reshape(length, head_count * HEAD_DIM) * jax.nn.silu(z_gate.astype(jnp.float32))
    grouped = gated.reshape(length, group_count, INNER // GROUPS)
    scaled = grouped * lax.rsqrt(jnp.mean(grouped * grouped, axis=-1, keepdims=True) + epsilon)
    normed_inner = (scaled.reshape(length, head_count * HEAD_DIM) * norm_gain).astype(jnp.bfloat16)
    rows = length // lax.axis_size("head")
    summed = lax.psum_scatter(
        jnp.dot(normed_inner, w_out, preferred_element_type=jnp.float32),
        "head",
        scatter_dimension=0,
        tiled=True,
    )
    hidden_out = residual.astype(jnp.float32) + summed
    normed = (
        hidden_out
        * lax.rsqrt(jnp.mean(hidden_out * hidden_out, axis=-1, keepdims=True) + epsilon)
        * final_gain
    ).astype(jnp.bfloat16)
    token_all = lax.all_gather(normed, "seq", axis=0, tiled=True)
    wanted = targets.reshape(-1)
    offset = lax.axis_index("seq") * (vocab.shape[0] * lax.axis_size("head"))
    update = vocab_fold(token_all, wanted, offset)
    top, total, picked = update(
        start_triple(token_all.shape[0]),
        lax.all_gather(vocab, "head", axis=0, tiled=True),
        jnp.int32(0),
    )
    top, total, picked = joined((top, total, picked), "seq", combine)
    every = picked - top - jnp.log(total)
    logprob = lax.dynamic_slice_in_dim(every, lax.axis_index("seq") * rows, rows, 0)
    return (hidden_out, logprob)


def solution(mesh):
    return jax.shard_map(
        shards,
        mesh=mesh,
        in_specs=(
            P("seq", "head"),
            P("seq", "head"),
            P("seq", "head"),
            P("seq", "head"),
            P("seq", "head"),
            P("seq", "head"),
            P("head"),
            P("head"),
            P("head", None),
            P(("seq", "head"), None),
            P(),
            P(("seq", "head"), None),
            P(None, "head"),
        ),
        out_specs=(P(("seq", "head"), None), P(("seq", "head"))),
        check_vma=False,
    )
```

profile of v0, /device:TPU:2, one launch (start us, length us, event | category | flops | bytes accessed | tf_op | source)
XLA Modules:
  0.0 679.8 jit_solution(15846469999163818144)
XLA Ops:
  7.2 0.8 copy.32
  8.0 0.2 reduce_window_sum.11
  8.2 0.8 copy.37
  9.1 1.1 copy.35
  10.3 0.9 convert_element_type.20
  11.1 2.0 fusion.5
  13.2 0.1 copy.33
  13.3 0.9 convert_element_type.21
  14.2 43.4 %all-gather.3 = f32[32,1,16]{2,1,0:T(1,128)S(1)} all-gather(f32[1,1,16]{2,1,0:T(1,128)S(1)} %get-tuple-element.331), channel_id=1, replica_groups=mesh['seq'=32,'head'=8] {'seq'}, dimensions={0}, use_global_device_ids=true | all-gather | bytes 2112 | tf_op jit(solution)/shard_map/all_gather | solution.py:19
  57.6 0.1 fusion.30
  57.8 1.4 convolution_bitcast_fusion.1
  59.2 190.0 %all-gather.15.cloned.1.call-done = f32[512,64,256]{2,1,0:T(8,128)} async-done(((f32[16,64,256]{2,1,0:T(8,128)}), f32[512,64,256]{2,1,0:T(8,128)}) %all-gather.15.cloned.1.call-update) | async-done | bytes 33554448 | tf_op jit(solution)/shard_map/all_gather | solution.py:19
  249.2 48.2 %while.34 = (s32[]{:T(128)}, f32[16,64,256]{2,1,0:T(8,128)S(1)}, s32[]{:T(128)}, f32[32,16]{1,0:T(8,128)S(1)}, f32[32,16,64,256]{3,2,1,0:T(8,128)}, /*index=5*/s32[]{:T(128)}, s32[]{:T(128)}) while((s32[]{:T(128)}, f32[16,64,256]{2,1,0:T(8,128)S(1)}, s32[]{:T(128)}, f32[32,16]{1,0:T(8,128)S(1)}, f32[32,16,64,256]{3,2,1,0:T(8,128)}, ...), condition=%wide.region_2.3_spmd.clone, body=%wide.region_1.2_spmd.clone.sunk | while | flops 1048580 | bytes 3146025 | solution.py:31
  249.2 1.5 fusion.39
  250.7 1.5 fusion.39
  252.2 1.5 fusion.39
  253.7 1.5 fusion.39
  255.2 1.5 fusion.39
  256.7 1.5 fusion.39
  258.3 1.5 fusion.39
  259.8 1.5 fusion.39
  261.3 1.5 fusion.39
  262.8 1.5 fusion.39
  264.3 1.5 fusion.39
  265.8 1.5 fusion.39
  267.3 1.5 fusion.39
  268.8 1.5 fusion.39
  270.3 1.5 fusion.39
  271.8 1.5 fusion.39
  273.3 1.5 fusion.39
  274.8 1.5 fusion.39
  276.3 1.5 fusion.39
  277.8 1.5 fusion.39
  279.3 1.5 fusion.39
  280.8 1.5 fusion.39
  282.3 1.5 fusion.39
  283.8 1.5 fusion.39
  285.3 1.5 fusion.39
  286.8 1.5 fusion.39
  288.3 1.5 fusion.39
  289.9 1.5 fusion.39
  291.4 1.5 fusion.39
  292.9 1.5 fusion.39
  294.4 1.5 fusion.39
  295.9 1.5 fusion.39
  297.4 2.3 fusion.3
  299.6 0.2 copy.39
  299.9 0.3 multiply_reduce_fusion
  300.1 6.1 fusion.23
  306.3 0.7 all-gather.13.cloned.1.call-update
  307.1 29.6 %reduce-scatter.2.cloned.1.call-done = f32[16,4096]{1,0:T(8,128)} async-done(((f32[128,4096]{1,0:T(8,128)}), f32[16,4096]{1,0:T(8,128)}) %reduce-scatter.2.cloned.1.call-update) | async-done | bytes 262160 | tf_op jit(solution)/shard_map/reduce_scatter | solution.py:144
  336.6 1.1 multiply_reduce_fusion.1
  337.8 0.7 multiply_convert_fusion.2
  338.6 0.1 copy.40
  338.6 0.1 eq.16
  338.7 89.0 %all-gather.13.cloned.1.call-done = bf16[2048,4096]{1,0:T(8,128)(2,1)} async-done(((bf16[256,4096]{1,0:T(8,128)(2,1)}), bf16[2048,4096]{1,0:T(8,128)(2,1)}) %all-gather.13.cloned.1.call-update) | async-done | bytes 16777232 | tf_op jit(solution)/shard_map/all_gather | solution.py:162
  427.8 85.3 %all-gather.11.cloned.1.call-done = bf16[512,4096]{1,0:T(8,128)(2,1)} async-done(((bf16[16,4096]{1,0:T(8,128)(2,1)}), bf16[512,4096]{1,0:T(8,128)(2,1)}) %all-gather.11.cloned.1.call-update) | async-done | bytes 4194320 | tf_op jit(solution)/shard_map/all_gather | solution.py:156
  513.0 13.3 %fusion.29 = (f32[512]{0:T(512)S(1)}, f32[512,2048]{1,0:T(8,128)S(1)}) fusion(bf16[512,4096]{1,0:T(8,128)(2,1)} %all-gather.11.cloned.1.call-done, bf16[2048,4096]{1,0:T(8,128)(2,1)} %all-gather.13.cloned.1.call-done), kind=kOutput, calls=%fused_computation.60 | convolution fusion | flops 8590983168 | bytes 25167872 | tf_op jit(solution)/shard_map/dot_general | solution.py:81
  526.3 1.2 select_reduce_fusion
  527.5 47.6 %all-gather.5 = f32[32,1,512]{2,1,0:T(1,128)S(1)} all-gather(f32[1,1,512]{2,1,0:T(1,128)S(1)} %bitcast.80), channel_id=1, replica_groups=mesh['seq'=32,'head'=8] {'seq'}, dimensions={0}, use_global_device_ids=true | all-gather | bytes 67584 | tf_op jit(solution)/shard_map/all_gather | solution.py:35
  575.1 47.0 %all-gather.6 = f32[32,1,512]{2,1,0:T(1,128)S(1)} all-gather(f32[1,1,512]{2,1,0:T(1,128)S(1)} %bitcast.78), channel_id=4, replica_groups=mesh['seq'=32,'head'=8] {'seq'}, dimensions={0}, use_global_device_ids=true | all-gather | bytes 67584 | tf_op jit(solution)/shard_map/all_gather | solution.py:35
  622.1 47.6 %all-gather.4 = f32[32,1,512]{2,1,0:T(1,128)S(1)} all-gather(f32[1,1,512]{2,1,0:T(1,128)S(1)} %bitcast.76), channel_id=3, replica_groups=mesh['seq'=32,'head'=8] {'seq'}, dimensions={0}, use_global_device_ids=true | all-gather | bytes 67584 | tf_op jit(solution)/shard_map/all_gather | solution.py:35
  669.7 2.9 while.33
  672.7 0.6 dynamic_slice.60
  (200 shorter events, 2.5 us)
Async XLA Ops:
  7.2 50.6 %copy-start.6 = (f32[128,16]{0,1:T(8,128)S(1)}, f32[128,16]{0,1:T(8,128)}, u32[]{:S(2)}) copy-start(f32[128,16]{0,1:T(8,128)} %param.22) | copy-start | bytes 24580
  7.2 50.4 %copy-start.1 = (bf16[128,256]{1,0:T(8,128)(2,1)S(1)}, bf16[128,256]{1,0:T(8,128)(2,1)}, u32[]{:S(2)}) copy-start(bf16[128,256]{1,0:T(8,128)(2,1)} %param.19) | copy-start | bytes 196612
  7.2 50.4 %copy-start.2 = (bf16[128,256]{1,0:T(8,128)(2,1)S(1)}, bf16[128,256]{1,0:T(8,128)(2,1)}, u32[]{:S(2)}) copy-start(bf16[128,256]{1,0:T(8,128)(2,1)} %param.20) | copy-start | bytes 196612
  7.2 242.0 %all-gather.15.cloned.1.call-start = ((), (), s32[]{:S(2)}) async-start(), calls=%async_computation.4 | async-start | bytes 34603008 | tf_op jit(solution)/shard_map/all_gather | solution.py:19
  13.1 323.5 %reduce-scatter.2.cloned.1.call-start = ((), (), s32[]{:S(2)}) async-start(), calls=%async_computation.1 | async-start | bytes 2359296 | tf_op jit(solution)/shard_map/reduce_scatter | solution.py:144
  249.2 48.2 %copy-start.8 = (f32[16]{0:T(128)S(1)}, f32[16]{0:T(128)}, u32[]{:S(2)}) copy-start(f32[16]{0:T(128)} %param.23) | copy-start | bytes 196
  249.2 50.7 %copy-start.3 = (bf16[128,1024]{1,0:T(8,128)(2,1)S(1)}, bf16[128,1024]{1,0:T(8,128)(2,1)}, u32[]{:S(2)}) copy-start(bf16[128,1024]{1,0:T(8,128)(2,1)} %param.18) | copy-start | bytes 786436
  297.3 2.8 copy-start.9
  306.3 30.4 %copy-start.4 = (bf16[16,4096]{1,0:T(8,128)(2,1)S(1)}, bf16[16,4096]{1,0:T(8,128)(2,1)}, u32[]{:S(2)}) copy-start(bf16[16,4096]{1,0:T(8,128)(2,1)} %param.26) | copy-start | bytes 393220
  306.3 31.5 %copy-start.5 = (f32[4096]{0:T(1024)S(1)}, f32[4096]{0:T(1024)}, u32[]{:S(2)}) copy-start(f32[4096]{0:T(1024)} %param.27) | copy-start | bytes 49156
  306.3 32.3 %copy-start.7 = (s32[32,16]{0,1:T(8,128)S(1)}, s32[32,16]{0,1:T(8,128)}, u32[]{:S(2)}) copy-start(s32[32,16]{0,1:T(8,128)} %param.29) | copy-start | bytes 6148
  306.3 121.5 %all-gather.13.cloned.1.call-start = ((), (), s32[]{:S(2)}) async-start(), calls=%async_computation.3 | async-start | bytes 18874368 | tf_op jit(solution)/shard_map/all_gather | solution.py:162
  307.0 206.0 %all-gather.11.cloned.1.call-start = ((), (), s32[]{:S(2)}) async-start(), calls=%async_computation.2 | async-start | bytes 4325376 | tf_op jit(solution)/shard_map/all_gather | solution.py:156
  337.8 188.5 %copy-start = (f32[16,4096]{1,0:T(8,128)}, f32[16,4096]{1,0:T(8,128)S(1)}, u32[]{:S(2)}) copy-start(f32[16,4096]{1,0:T(8,128)S(1)} %get-tuple-element.325) | copy-start | bytes 786436
Sparse Core Ops, SparseCore 0:
  13.2 235.8 all-gather.14
  306.4 30.1 reduce-scatter.1
  338.5 89.1 all-gather.12
  430.2 82.7 all-gather.10
where the time goes:
time: 681 us; the launch traced here: 680 us
  waiting for transfers between devices  395 us (58%)
  blocking collectives  186 us (27%)
  other arithmetic  53.1 us (8%)
  matrix products  25.1 us (4%)
  between operations  14 us (2%)
    all_gather x1, waiting for transfers between devices, carried_in(): everything = jax.tree.map(lambda part: lax.all_gather(part, axis), value)  190 us
    all_gather x3, blocking collectives, joined(): gathered = jax.tree.map(lambda a: lax.all_gather(a, axis), part)  142 us
    all_gather x1, waiting for transfers between devices, shards(): lax.all_gather(vocab, 'head', axis=0, tiled=True)  89 us
    all_gather x1, waiting for transfers between devices, shards(): token_all = lax.all_gather(normed, 'seq', axis=0, tiled=True)  85.3 us
    select_n x32, other arithmetic, hop(): return jax.tree.map(lambda a, b: jnp.where(reached, a, b), new, before)  46.9 us
    all_gather x1, blocking collectives, carried_in(): everything = jax.tree.map(lambda part: lax.all_gather(part, axis), value)  43.4 us
    reduce_scatter x1, waiting for transfers between devices, shards(): lax.psum_scatter(jnp.dot(normed_inner, w_out, preferred_element_type=jnp....  29.6 us
  transfers between devices with their start and end apart: 4, of which 4 were waited for; matrix products, arithmetic and copies ran while one was open for 1% of the time, Pallas kernels for 0%

commit v1 on v0

v1 whole, which is shorter than its diff:
```python
import jax
import jax.numpy as jnp
from jax import lax
from jax.experimental import pallas as pl
from jax.experimental.pallas import tpu as pltpu
from jax.sharding import Mesh, PartitionSpec as P

HEAD_DIM = 64
STATE = 256
CHAN = 1024
BLOCKS = 32
SLICE = STATE // BLOCKS
EXTRA = 128
HALF = jnp.float16
PART_SCALE = 512.0
TILE = 512

epsilon = 1e-05
highest = lax.Precision.HIGHEST
SEQ = ("z", "y")
HEAD = ("x", "core")


def pieces(value):
    value = value * 128.0
    first = lax.reduce_precision(value, 5, 10)
    second = lax.reduce_precision(value - first, 5, 10)
    third = value - first - second
    return [part.astype(HALF) for part in (first, second, third)]


def scan_kernel(recv_ref, out_ref):
    head_of = lax.broadcasted_iota(jnp.int32, (EXTRA, CHAN), 1) // HEAD_DIM
    spread = (head_of == lax.broadcasted_iota(jnp.int32, (EXTRA, CHAN), 0)).astype(jnp.float32)
    wide = jnp.dot(
        recv_ref[:, CHAN:],
        spread,
        precision=highest,
        preferred_element_type=jnp.float32,
    )
    state = jnp.zeros((SLICE, CHAN), jnp.float32)
    for block in range(BLOCKS):
        rows = slice(block * SLICE, (block + 1) * SLICE)
        out_ref[rows, :] = state
        last = wide[rows, :]
        decay = jnp.exp((last[0:1] + last[1:2] + last[2:3]) * (-1.0 / 128.0))
        state = decay * state + recv_ref[rows, :CHAN]


def scan_states(received):
    return pl.pallas_call(
        scan_kernel,
        out_shape=jax.ShapeDtypeStruct((STATE, CHAN), jnp.float32),
        name="scan_states",
    )(received.astype(jnp.float32)).astype(HALF)


def score_kernel(wanted_ref, token_ref, vocab_ref, out_ref, top_ref, total_ref, hit_ref):
    step = pl.program_id(0)
    count = token_ref.shape[0]

    @pl.when(step == 0)
    def _():
        top_ref[...] = jnp.full(top_ref.shape, -jnp.inf, jnp.float32)
        total_ref[...] = jnp.zeros(total_ref.shape, jnp.float32)
        hit_ref[...] = jnp.zeros(hit_ref.shape, jnp.float32)

    logits = lax.dot_general(
        vocab_ref[...],
        token_ref[...],
        (((1,), (1,)), ((), ())),
        preferred_element_type=jnp.float32,
    )
    ids = step * TILE + lax.broadcasted_iota(jnp.int32, logits.shape, 0)
    hit = jnp.where(ids == wanted_ref[...], logits, 0.0)
    hit_ref[...] += jnp.sum(hit.reshape(TILE // 8, 8, count), axis=0)
    folded = logits.reshape(TILE // 8, 8, count)
    old = top_ref[...]
    new = jnp.maximum(old, jnp.max(folded, axis=0))
    top_ref[...] = new
    total_ref[...] = total_ref[...] * jnp.exp(old - new) + jnp.sum(
        jnp.exp(folded - new[None]), axis=0
    )

    @pl.when(step == pl.num_programs(0) - 1)
    def _():
        lane_top = top_ref[...]
        top = jnp.max(lane_top, axis=0, keepdims=True)
        total = jnp.sum(total_ref[...] * jnp.exp(lane_top - top), axis=0, keepdims=True)
        picked = jnp.sum(hit_ref[...], axis=0, keepdims=True)
        row = lax.broadcasted_iota(jnp.int32, (8, count), 0)
        out_ref[...] = jnp.where(row == 0, top, jnp.where(row == 1, total, picked))


def score(wanted, token, vocab):
    count, width = token.shape
    entries = vocab.shape[0]
    return pl.pallas_call(
        score_kernel,
        grid=(entries // TILE,),
        in_specs=[
            pl.BlockSpec((1, count), lambda i: (0, 0)),
            pl.BlockSpec((count, width), lambda i: (0, 0)),
            pl.BlockSpec((TILE, width), lambda i: (i, 0)),
        ],
        out_specs=pl.BlockSpec((8, count), lambda i: (0, 0)),
        out_shape=jax.ShapeDtypeStruct((8, count), jnp.float32),
        scratch_shapes=[pltpu.VMEM((8, count), jnp.float32)] * 3,
        cost_estimate=pl.CostEstimate(
            flops=2 * count * width * entries,
            bytes_accessed=2 * (count + entries) * width,
            transcendentals=count * entries,
        ),
        name="score",
    )(wanted, token, vocab)


def exchange(value, axes):
    return lax.all_to_all(value, axes, split_axis=0, concat_axis=0, tiled=True)


def inner(
    x_in,
    z_gate,
    b_in,
    c_in,
    log_decay,
    step_size,
    d_skip,
    norm_gain,
    w_out,
    residual,
    final_gain,
    vocab,
    targets,
):
    length = x_in.shape[0]
    heads = log_decay.shape[1]
    vocab_all = lax.all_gather(vocab, HEAD, axis=0, tiled=True)

    inputs = x_in.astype(jnp.float32)
    cumulative = jnp.cumsum(log_decay, axis=0)
    last = cumulative[-1]
    end_weight = jnp.exp(last[None, :] - cumulative) * step_size
    weighted = inputs * jnp.repeat(end_weight, HEAD_DIM, axis=1)
    end_state = lax.dot_general(
        b_in.astype(jnp.float32), weighted, (((0,), (0,)), ((), ())), precision=highest
    ).astype(HALF)
    side = jnp.stack(pieces(last))
    side = jnp.pad(side, ((0, SLICE - 3), (0, EXTRA - heads)))
    side = jnp.broadcast_to(side[None], (BLOCKS, SLICE, EXTRA))
    payload = jnp.concatenate([end_state.reshape(BLOCKS, SLICE, CHAN), side], axis=-1)
    received = exchange(payload.reshape(STATE, CHAN + EXTRA), SEQ)
    incoming = exchange(scan_states(received), SEQ)

    by_head = cumulative.T
    gaps = by_head[:, None, :] - by_head[:, :, None]
    positions = jnp.arange(length)
    causal = positions[None, :] <= positions[:, None]
    segment_w = jnp.where(causal[None], jnp.exp(jnp.minimum(gaps, 0.0)), 0.0)
    scores = lax.dot_general(
        c_in, b_in, (((1,), (1,)), ((), ())), preferred_element_type=jnp.float32
    )
    weights = segment_w * scores[None] * step_size.T[:, None, :]
    within = jnp.einsum(
        "hts,shp->thp", weights, inputs.reshape(length, heads, HEAD_DIM), precision=highest
    ).reshape(length, CHAN)
    local = within + jnp.repeat(d_skip, HEAD_DIM)[None, :] * inputs

    carried = jnp.dot(c_in.astype(jnp.float32), incoming.astype(jnp.float32), precision=highest)
    mixed = local + jnp.repeat(jnp.exp(-cumulative), HEAD_DIM, axis=1) * carried
    gated = mixed * jax.nn.silu(z_gate.astype(jnp.float32))
    scaled = gated * lax.rsqrt(jnp.mean(gated * gated, axis=-1, keepdims=True) + epsilon)
    normed_inner = (scaled * norm_gain).astype(jnp.bfloat16)
    partial = jnp.dot(normed_inner, w_out, preferred_element_type=jnp.float32)
    parts = exchange((partial * PART_SCALE).astype(HALF), HEAD)
    rows = length // 8
    summed = jnp.sum(parts.reshape(8, rows, -1).astype(jnp.float32), axis=0) * (1.0 / PART_SCALE)
    hidden_out = residual.astype(jnp.float32) + summed
    normed = (
        hidden_out
        * lax.rsqrt(jnp.mean(hidden_out * hidden_out, axis=-1, keepdims=True) + epsilon)
        * final_gain
    ).astype(jnp.bfloat16)

    half = rows // 2
    near_a = exchange(jnp.concatenate([normed[:half]] * 4, axis=0), "y")
    token_a = lax.all_gather(near_a, "z", axis=0, tiled=True)
    far_b = exchange(jnp.concatenate([normed[half:]] * 8, axis=0), "z")
    token_b = exchange(jnp.concatenate([far_b] * 4, axis=0), "y")

    offset = lax.axis_index(SEQ) * vocab_all.shape[0]
    wanted = (targets - offset).reshape(8, 4, rows)
    wanted_a = wanted[:, :, :half].reshape(1, -1)
    wanted_b = wanted[:, :, half:].transpose(1, 0, 2).reshape(1, -1)
    found_a = score(wanted_a, token_a, vocab_all)
    found_b = score(wanted_b, token_b, vocab_all)
    found_a = found_a.reshape(8, 8, 4, half)
    found_b = found_b.reshape(8, 4, 8, half).transpose(0, 2, 1, 3)
    triple = jnp.concatenate([found_a, found_b], axis=-1).reshape(8, BLOCKS, rows)
    triple = jnp.pad(triple.transpose(1, 0, 2), ((0, 0), (0, 0), (0, 128 - rows)))
    triples = exchange(triple.reshape(BLOCKS * 8, 128), SEQ)
    triples = triples.reshape(BLOCKS, 8, 128)[:, :3, :rows]
    tops, totals, picks = triples[:, 0], triples[:, 1], triples[:, 2]
    best = jnp.max(tops, axis=0)
    whole = jnp.sum(totals * jnp.exp(tops - best[None]), axis=0)
    logprob = jnp.sum(picks, axis=0) - best - jnp.log(whole)
    return (hidden_out, logprob)


def solution(mesh):
    fine = Mesh(mesh.devices.reshape(8, 4, 4, 2), ("z", "y", "x", "core"))
    return jax.shard_map(
        inner,
        mesh=fine,
        in_specs=(
            P(SEQ, HEAD),
            P(SEQ, HEAD),
            P(SEQ, HEAD),
            P(SEQ, HEAD),
            P(SEQ, HEAD),
            P(SEQ, HEAD),
            P(HEAD),
            P(HEAD),
            P(HEAD, None),
            P(SEQ + HEAD, None),
            P(),
            P(SEQ + HEAD, None),
            P(None, HEAD),
        ),
        out_specs=(P(SEQ + HEAD, None), P(SEQ + HEAD)),
        check_vma=False,
    )
```

time: 681 us -> 213 us (0.31)
  waiting for transfers between devices: 395 us -> 41.5 us
  blocking collectives: 186 us -> 98.8 us
  other arithmetic: 53.1 us -> 7.18 us
  Pallas kernels: 0 us -> 23.6 us
  matrix products: 25.1 us -> 8.06 us
  starting transfers between devices: 0.16 us -> 12.1 us
    all_gather x3 -> x2, waiting for transfers between devices: 364 us -> 0.02 us  [the longest x1 0.02 us: inner(): token_a = lax.all_gather(near_a, 'z', axis=0, tiled=True)]
    all_gather x4 -> x0, blocking collectives: 186 us -> none  [the longest x3 142 us: joined(): gathered = jax.tree.map(lambda a: lax.all_gather(a, axis), part)]
    all_to_all x0 -> x4, blocking collectives: none -> 98.8 us  [exchange(): return lax.all_to_all(value, axes, split_axis=0, concat_axis=0, tiled=True)]
    select_n x32 -> x0, other arithmetic: 46.9 us -> none  [hop(): return jax.tree.map(lambda a, b: jnp.where(reached, a, b), new, before)]
    all_to_all x0 -> x3, waiting for transfers between devices: none -> 40.8 us  [exchange(): return lax.all_to_all(value, axes, split_axis=0, concat_axis=0, tiled=True)]
    reduce_scatter x1 -> x0, waiting for transfers between devices: 29.6 us -> none  [shards(): lax.psum_scatter(jnp.dot(normed_inner, w_out, preferred_element_type=jnp....]
    pallas_call x0 -> x3, Pallas kernels: none -> 23.6 us  [the longest x2 20.2 us: score(): pl.pallas_call(score_kernel, grid=(entries // TILE,), in_specs=[pl.BlockS...]
    dot_general x6 -> x5, matrix products: 25.1 us -> 8.06 us  [the longest x1 4.98 us: inner(): partial = jnp.dot(normed_inner, w_out, preferred_element_type=jnp.float32)]
  transfers between devices with their start and end apart: 4 -> 5, of which waited for: 4 -> 3; matrix products, arithmetic and copies ran while one was open for 1% -> 8% of each run, Pallas kernels for 0% -> 6%
where the time goes in v1:
time: 213 us; the launch traced here: 212 us
  blocking collectives  98.8 us (46%)
  waiting for transfers between devices  41.5 us (19%)
  Pallas kernels  23.6 us (11%)
  between operations  14.4 us (7%)
  starting transfers between devices  12.1 us (6%)
  matrix products  8.06 us (4%)
  other arithmetic  7.18 us (3%)
  local copies, waits for them, and re-layouts  6.37 us (3%)
    all_to_all x4, blocking collectives, exchange(): return lax.all_to_all(value, axes, split_axis=0, concat_axis=0, tiled=True)  98.8 us
    all_to_all x3, waiting for transfers between devices, exchange(): return lax.all_to_all(value, axes, split_axis=0, concat_axis=0, tiled=True)  40.8 us
    pallas_call x2, Pallas kernels, score(): pl.pallas_call(score_kernel, grid=(entries // TILE,), in_specs=[pl.BlockS...  20.2 us
    all_to_all x3, starting transfers between devices, exchange(): return lax.all_to_all(value, axes, split_axis=0, concat_axis=0, tiled=True)  12.1 us
    dot_general x1, matrix products, inner(): partial = jnp.dot(normed_inner, w_out, preferred_element_type=jnp.float32)  4.98 us
  transfers between devices with their start and end apart: 5, of which 3 were waited for; matrix products, arithmetic and copies ran while one was open for 8% of the time, Pallas kernels for 6%

profile of v1, /device:TPU:2, one launch (start us, length us, event | category | flops | bytes accessed | tf_op | source)
XLA Modules:
  0.0 212.0 jit_solution(14659262458755721423)
XLA Ops:
  7.2 0.0 copy-start
  7.2 0.0 copy-start.11
  7.2 0.0 copy-start.10
  7.2 0.0 copy-start.4
  7.2 0.0 all-gather.5.cloned.1.call-start
  7.3 0.7 all-gather.5.cloned.1.call-update
  7.9 0.0 copy-done.11
  8.0 0.1 copy.45
  8.1 0.1 copy.39
  8.2 0.2 reduce_window_sum.11
  8.4 0.1 copy.46
  8.4 0.2 copy.42
  8.7 0.6 fusion.1
  9.4 0.1 pad_maximum_fusion.1
  9.5 30.3 %all_to_all.68 = f16[32,8,1152]{2,1,0:T(8,128)(2,1)S(1)} all-to-all(f16[32,8,1152]{2,1,0:T(8,128)(2,1)S(1)} %pad_maximum_fusion.1), channel_id=1, replica_groups=mesh['z'=8,'y'=4,'x'=4,'core'=2] {'z','y'}, dimensions={0} | all-to-all | bytes 1179648 | tf_op jit(solution)/shard_map/all_to_all | solution.py:119
  39.8 1.1 bitcast_convert_fusion.recv_ref
  40.9 3.4 %scan_states.1 = f32[256,1024]{1,0:T(8,128)} custom-call(f32[256,1152]{1,0:T(8,128)} %bitcast_convert_fusion.recv_ref), custom_call_target="tpu_custom_call" | custom-call | tf_op jit(solution)/shard_map/scan_states/pallas_call | solution.py:51
  44.3 2.2 %convert_bitcast_fusion = f16[32,8,1024]{2,1,0:T(8,128)(2,1)} fusion(f32[256,1024]{1,0:T(8,128)} %scan_states.1), kind=kLoop, calls=%fused_computation.30 | loop fusion | flops 262144 | bytes 1572864 | tf_op jit(solution)/shard_map/all_to_all | solution.py:119
  46.5 4.7 %all-to-all-start.1 = ((f16[32,8,1024]{2,1,0:T(8,128)(2,1)}), f16[32,8,1024]{2,1,0:T(8,128)(2,1)S(1)}, u32[]{:S(2)}, u32[]{:S(2)}) async-start(f16[32,8,1024]{2,1,0:T(8,128)(2,1)} %convert_bitcast_fusion), calls=%async_computation.1 | async-start | bytes 1048576 | tf_op jit(solution)/shard_map/all_to_all | solution.py:119
  51.3 0.2 copy.47
  51.4 0.1 copy.44
  51.5 0.1 copy.40
  51.6 0.0 copy-done.13
  51.6 0.1 broadcast_in_dim.19
  51.6 0.1 mul.111
  51.8 0.0 copy-done.8
  51.8 0.1 fusion.38
  51.9 1.4 fusion.5
  53.3 0.0 copy-start.7
  53.3 15.0 %all-to-all-done.1 = f16[32,8,1024]{2,1,0:T(8,128)(2,1)S(1)} async-done(((f16[32,8,1024]{2,1,0:T(8,128)(2,1)}), f16[32,8,1024]{2,1,0:T(8,128)(2,1)S(1)}, u32[]{:S(2)}, u32[]{:S(2)}) %all-to-all-start.1) | async-done | bytes 524320 | tf_op jit(solution)/shard_map/all_to_all | solution.py:119
  68.4 0.9 multiply_reduce_fusion
  69.3 5.0 %fusion = f16[128,4096]{1,0:T(8,128)(2,1)S(1)} fusion(bf16[1024,4096]{1,0:T(8,128)(2,1)} %param.21, f32[128,1024]{0,1:T(8,128)S(1)} %get-tuple-element.18, f32[1024]{0:T(1024)S(1)} %copy-done.7, f32[128]{0:T(128)S(1)} %add_rsqrt_fusion.1), kind=kOutput, calls=%fused_computation.1 | convolution fusion | flops 1075183616 | bytes 9966080 | tf_op jit(solution)/shard_map/dot_general | solution.py:175
  74.3 0.0 copy-start.6
  74.3 0.0 copy-start.9
  74.3 30.8 %all_to_all.69 = f16[8,16,4096]{2,1,0:T(8,128)(2,1)S(1)} all-to-all(f16[8,16,4096]{2,1,0:T(8,128)(2,1)S(1)} %bitcast.60), channel_id=1, replica_groups=mesh['z'=8,'y'=4,'x'=4,'core'=2] {'x','core'}, dimensions={0} | all-to-all | bytes 2097152 | tf_op jit(solution)/shard_map/all_to_all | solution.py:119
  105.2 0.2 convert_reduce_fusion
  105.3 0.0 copy-done.6
  105.3 0.2 multiply_reduce_fusion.1
  105.5 0.1 multiply_convert_fusion.2
  105.7 0.7 maximum_bitcast_fusion
  106.4 3.6 %all-to-all-start.3 = ((bf16[4,8,4096]{2,1,0:T(8,128)(2,1)}), bf16[4,8,4096]{2,1,0:T(8,128)(2,1)S(1)}, u32[]{:S(2)}, u32[]{:S(2)}) async-start(bf16[4,8,4096]{2,1,0:T(8,128)(2,1)} %maximum_bitcast_fusion), calls=%async_computation.3 | async-start | bytes 524288 | tf_op jit(solution)/shard_map/all_to_all | solution.py:119
  110.1 6.6 %all-to-all-done.3 = bf16[4,8,4096]{2,1,0:T(8,128)(2,1)S(1)} async-done(((bf16[4,8,4096]{2,1,0:T(8,128)(2,1)}), bf16[4,8,4096]{2,1,0:T(8,128)(2,1)S(1)}, u32[]{:S(2)}, u32[]{:S(2)}) %all-to-all-start.3) | async-done | bytes 262176 | tf_op jit(solution)/shard_map/all_to_all | solution.py:119
  116.7 0.7 copy-done.3
  117.4 0.0 all-gather.3.cloned.1.call-update
  117.4 22.9 %all_to_all.70 = bf16[8,8,4096]{2,1,0:T(8,128)(2,1)S(1)} all-to-all(bf16[8,8,4096]{2,1,0:T(8,128)(2,1)S(1)} %bitcast.65), channel_id=1, replica_groups=mesh['z'=8,'y'=4,'x'=4,'core'=2] {'z'}, dimensions={0} | all-to-all | bytes 1048576 | tf_op jit(solution)/shard_map/all_to_all | solution.py:119
  140.3 1.6 pad_maximum_fusion
  141.9 3.7 %all-to-all-start.5 = ((bf16[4,64,4096]{2,1,0:T(8,128)(2,1)}), bf16[4,64,4096]{2,1,0:T(8,128)(2,1)S(1)}, u32[]{:S(2)}, u32[]{:S(2)}) async-start(bf16[4,64,4096]{2,1,0:T(8,128)(2,1)} %bitcast.59), calls=%async_computation.5 | async-start | bytes 4194304 | tf_op jit(solution)/shard_map/all_to_all | solution.py:119
  145.6 0.1 copy.48
  145.7 0.1 fusion.37
  145.8 0.7 reshape.107.wanted_ref
  146.5 0.7 reshape.106.wanted_ref
  147.2 19.2 %all-to-all-done.5 = bf16[4,64,4096]{2,1,0:T(8,128)(2,1)S(1)} async-done(((bf16[4,64,4096]{2,1,0:T(8,128)(2,1)}), bf16[4,64,4096]{2,1,0:T(8,128)(2,1)S(1)}, u32[]{:S(2)}, u32[]{:S(2)}) %all-to-all-start.5) | async-done | bytes 2097184 | tf_op jit(solution)/shard_map/all_to_all | solution.py:119
  166.3 1.3 copy-done.1
  167.6 10.1 %score.3 = f32[8,256]{1,0:T(8,128)} custom-call(s32[1,256]{1,0:T(1,128)} %reshape.107.wanted_ref, bf16[256,4096]{1,0:T(8,128)(2,1)} %bitcast.58, bf16[2048,4096]{1,0:T(8,128)(2,1)} %all-gather.5.cloned.1.call-done.vocab_ref), custom_call_target="tpu_custom_call" | custom-call | flops 4294967296 | bytes 18874368 | tf_op jit(solution)/shard_map/score/pallas_call | solution.py:98
  177.7 0.8 reshape.108
  178.5 0.1 copy.50
  178.6 0.0 all-gather.3.cloned.1.call-done.token_ref
  178.7 10.1 %score.2 = f32[8,256]{1,0:T(8,128)} custom-call(s32[1,256]{1,0:T(1,128)} %reshape.106.wanted_ref, bf16[256,4096]{1,0:T(8,128)(2,1)} %all-gather.3.cloned.1.call-done.token_ref, bf16[2048,4096]{1,0:T(8,128)(2,1)} %all-gather.5.cloned.1.call-done.vocab_ref), custom_call_target="tpu_custom_call" | custom-call | flops 4294967296 | bytes 18874368 | tf_op jit(solution)/shard_map/score/pallas_call | solution.py:98
  188.7 0.8 concatenate.27
  189.5 0.1 maximum_bitcast_fusion.1
  189.7 0.1 copy.55
  189.8 14.8 %all_to_all.71 = f32[32,8,128]{2,1,0:T(8,128)S(1)} all-to-all(f32[32,8,128]{2,1,0:T(8,128)S(1)} %pad.9.clone), channel_id=1, replica_groups=mesh['z'=8,'y'=4,'x'=4,'core'=2] {'z','y'}, dimensions={0} | all-to-all | bytes 262144 | tf_op jit(solution)/shard_map/all_to_all | solution.py:119
  204.5 0.1 slice_reduce_fusion
  204.7 0.5 log_subtract_fusion
  (40 shorter events, 0.4 us)
Async XLA Ops:
  7.2 1.5 copy-start
  7.2 0.8 copy-start.11
  7.2 0.9 copy-start.10
  7.2 1.2 copy-start.4
  7.2 159.1 %all-gather.5.cloned.1.call-start = ((), (), s32[]{:S(2)}) async-start(), calls=%async_computation.8 | async-start | bytes 18874368 | tf_op jit(solution)/shard_map/all_gather | solution.py:139
  40.9 10.3 %copy-start.5 = (bf16[128,1024]{1,0:T(8,128)(2,1)S(1)}, bf16[128,1024]{1,0:T(8,128)(2,1)}, u32[]{:S(2)}) copy-start(bf16[128,1024]{1,0:T(8,128)(2,1)} %param.14) | copy-start | bytes 786436
  44.3 7.2 %copy-start.13 = (f32[16]{0:T(128)S(1)}, f32[16]{0:T(128)}, u32[]{:S(2)}) copy-start(f32[16]{0:T(128)} %param.19) | copy-start | bytes 196
  44.3 7.4 %copy-start.8 = (bf16[128,256]{1,0:T(8,128)(2,1)S(1)}, bf16[128,256]{1,0:T(8,128)(2,1)}, u32[]{:S(2)}) copy-start(bf16[128,256]{1,0:T(8,128)(2,1)} %param.16) | copy-start | bytes 196612
  46.5 21.9 %all-to-all-start.1 = ((f16[32,8,1024]{2,1,0:T(8,128)(2,1)}), f16[32,8,1024]{2,1,0:T(8,128)(2,1)S(1)}, u32[]{:S(2)}, u32[]{:S(2)}) async-start(f16[32,8,1024]{2,1,0:T(8,128)(2,1)} %convert_bitcast_fusion), calls=%async_computation.1 | async-start | bytes 1048576 | tf_op jit(solution)/shard_map/all_to_all | solution.py:119
  53.3 16.0 %copy-start.7 = (f32[1024]{0:T(1024)S(1)}, f32[1024]{0:T(1024)}, u32[]{:S(2)}) copy-start(f32[1024]{0:T(1024)} %param.20) | copy-start | bytes 12292
  74.3 31.0 %copy-start.6 = (bf16[16,4096]{1,0:T(8,128)(2,1)S(1)}, bf16[16,4096]{1,0:T(8,128)(2,1)}, u32[]{:S(2)}) copy-start(bf16[16,4096]{1,0:T(8,128)(2,1)} %param.22) | copy-start | bytes 393220
  74.3 31.2 %copy-start.9 = (f32[4096]{0:T(1024)S(1)}, f32[4096]{0:T(1024)}, u32[]{:S(2)}) copy-start(f32[4096]{0:T(1024)} %param.23) | copy-start | bytes 49156
  105.5 36.4 %copy-start.2 = (f32[16,4096]{1,0:T(8,128)}, f32[16,4096]{1,0:T(8,128)S(1)}, u32[]{:S(2)}) copy-start(f32[16,4096]{1,0:T(8,128)S(1)} %get-tuple-element.3) | copy-start | bytes 786436
  106.4 10.3 %all-to-all-start.3 = ((bf16[4,8,4096]{2,1,0:T(8,128)(2,1)}), bf16[4,8,4096]{2,1,0:T(8,128)(2,1)S(1)}, u32[]{:S(2)}, u32[]{:S(2)}) async-start(bf16[4,8,4096]{2,1,0:T(8,128)(2,1)} %maximum_bitcast_fusion), calls=%async_computation.3 | async-start | bytes 524288 | tf_op jit(solution)/shard_map/all_to_all | solution.py:119
  110.0 68.6 %all-gather.3.cloned.1.call-start = ((), (), s32[]{:S(2)}) async-start(), calls=%async_computation.7 | async-start | bytes 2359296 | tf_op jit(solution)/shard_map/all_gather | solution.py:188
  116.7 0.7 copy-start.3
  141.9 3.8 %copy-start.12 = (s32[32,16]{0,1:T(8,128)S(1)}, s32[32,16]{0,1:T(8,128)}, u32[]{:S(2)}) copy-start(s32[32,16]{0,1:T(8,128)} %param.25) | copy-start | bytes 6148
  141.9 24.4 %all-to-all-start.5 = ((bf16[4,64,4096]{2,1,0:T(8,128)(2,1)}), bf16[4,64,4096]{2,1,0:T(8,128)(2,1)S(1)}, u32[]{:S(2)}, u32[]{:S(2)}) async-start(bf16[4,64,4096]{2,1,0:T(8,128)(2,1)} %bitcast.59), calls=%async_computation.5 | async-start | bytes 4194304 | tf_op jit(solution)/shard_map/all_to_all | solution.py:119
  166.3 1.3 copy-start.1
Sparse Core Ops, SparseCore 0:
  9.9 101.2 all-gather.4
  117.5 41.5 all-gather.2

commit v2 on v1

--- a/solution.py
+++ b/solution.py
@@ -32,8 +32,9 @@
 def scan_kernel(recv_ref, out_ref):
     head_of = lax.broadcasted_iota(jnp.int32, (EXTRA, CHAN), 1) // HEAD_DIM
     spread = (head_of == lax.broadcasted_iota(jnp.int32, (EXTRA, CHAN), 0)).astype(jnp.float32)
-    wide = jnp.dot(
-        recv_ref[:, CHAN:],
+    last = jnp.sum(recv_ref[:, CHAN:].reshape(BLOCKS, SLICE, EXTRA), axis=1)
+    decay = jnp.dot(
+        jnp.exp(last * (-1.0 / 128.0)),
         spread,
         precision=highest,
         preferred_element_type=jnp.float32,
@@ -42,9 +43,7 @@
     for block in range(BLOCKS):
         rows = slice(block * SLICE, (block + 1) * SLICE)
         out_ref[rows, :] = state
-        last = wide[rows, :]
-        decay = jnp.exp((last[0:1] + last[1:2] + last[2:3]) * (-1.0 / 128.0))
-        state = decay * state + recv_ref[rows, :CHAN]
+        state = decay[block : block + 1] * state + recv_ref[rows, :CHAN]
 
 
 def scan_states(received):
@@ -55,7 +54,10 @@
     )(received.astype(jnp.float32)).astype(HALF)
 
 
-def score_kernel(wanted_ref, token_ref, vocab_ref, out_ref, top_ref, total_ref, hit_ref):
+def score_kernel(*refs):
+    wanted_ref, token_ref, vocab_ref = refs[:3]
+    near_ref = refs[3] if len(refs) == 8 else None
+    out_ref, top_ref, total_ref, hit_ref = refs[-4:]
     step = pl.program_id(0)
     count = token_ref.shape[0]
 
@@ -88,11 +90,21 @@
         top = jnp.max(lane_top, axis=0, keepdims=True)
         total = jnp.sum(total_ref[...] * jnp.exp(lane_top - top), axis=0, keepdims=True)
         picked = jnp.sum(hit_ref[...], axis=0, keepdims=True)
-        row = lax.broadcasted_iota(jnp.int32, (8, count), 0)
-        out_ref[...] = jnp.where(row == 0, top, jnp.where(row == 1, total, picked))
-
-
-def score(wanted, token, vocab):
+        row = lax.broadcasted_iota(jnp.int32, (128, count), 0) % 3
+        packed = jnp.where(row == 0, top, jnp.where(row == 1, total, picked)).T
+        if near_ref is None:
+            out_ref[...] = packed
+        else:
+            lane = lax.broadcasted_iota(jnp.int32, (8, 128), 1)
+            for z in range(8):
+                for y in range(4):
+                    there = pl.ds((z * 4 + y) * 8, 8)
+                    here = (y * 8 + z) * 8
+                    far = packed[here : here + 8]
+                    out_ref[there, :] = jnp.where(lane < 3, near_ref[there, :], far)
+
+
+def score(wanted, token, vocab, *near):
     count, width = token.shape
     entries = vocab.shape[0]
     return pl.pallas_call(
@@ -102,17 +114,19 @@
             pl.BlockSpec((1, count), lambda i: (0, 0)),
             pl.BlockSpec((count, width), lambda i: (0, 0)),
             pl.BlockSpec((TILE, width), lambda i: (i, 0)),
-        ],
-        out_specs=pl.BlockSpec((8, count), lambda i: (0, 0)),
-        out_shape=jax.ShapeDtypeStruct((8, count), jnp.float32),
+        ]
+        + [pl.BlockSpec((count, 128), lambda i: (0, 0))] * len(near),
+        out_specs=pl.BlockSpec((count, 128), lambda i: (0, 0)),
+        out_shape=jax.ShapeDtypeStruct((count, 128), jnp.float32),
         scratch_shapes=[pltpu.VMEM((8, count), jnp.float32)] * 3,
         cost_estimate=pl.CostEstimate(
             flops=2 * count * width * entries,
             bytes_accessed=2 * (count + entries) * width,
             transcendentals=count * entries,
         ),
+        compiler_params=pltpu.CompilerParams(vmem_limit_bytes=(48 if near else 52) * 2**20),
         name="score",
-    )(wanted, token, vocab)
+    )(wanted, token, vocab, *near)
 
 
 def exchange(value, axes):
@@ -173,9 +187,13 @@
     scaled = gated * lax.rsqrt(jnp.mean(gated * gated, axis=-1, keepdims=True) + epsilon)
     normed_inner = (scaled * norm_gain).astype(jnp.bfloat16)
     partial = jnp.dot(normed_inner, w_out, preferred_element_type=jnp.float32)
-    parts = exchange((partial * PART_SCALE).astype(HALF), HEAD)
     rows = length // 8
-    summed = jnp.sum(parts.reshape(8, rows, -1).astype(jnp.float32), axis=0) * (1.0 / PART_SCALE)
+    swapped = (partial * PART_SCALE).astype(HALF).reshape(4, 2, rows, -1).transpose(1, 0, 2, 3)
+    pair = exchange(swapped.reshape(length, -1), "core")
+    pair = pair.reshape(2, length // 2, -1).astype(jnp.float32)
+    pair = ((pair[0] + pair[1]) * 0.5).astype(HALF)
+    parts = exchange(pair, "x")
+    summed = jnp.sum(parts.reshape(4, rows, -1).astype(jnp.float32), axis=0) * (2.0 / PART_SCALE)
     hidden_out = residual.astype(jnp.float32) + summed
     normed = (
         hidden_out
@@ -194,18 +212,14 @@
     wanted_a = wanted[:, :, :half].reshape(1, -1)
     wanted_b = wanted[:, :, half:].transpose(1, 0, 2).reshape(1, -1)
     found_a = score(wanted_a, token_a, vocab_all)
-    found_b = score(wanted_b, token_b, vocab_all)
-    found_a = found_a.reshape(8, 8, 4, half)
-    found_b = found_b.reshape(8, 4, 8, half).transpose(0, 2, 1, 3)
-    triple = jnp.concatenate([found_a, found_b], axis=-1).reshape(8, BLOCKS, rows)
-    triple = jnp.pad(triple.transpose(1, 0, 2), ((0, 0), (0, 0), (0, 128 - rows)))
-    triples = exchange(triple.reshape(BLOCKS * 8, 128), SEQ)
-    triples = triples.reshape(BLOCKS, 8, 128)[:, :3, :rows]
-    tops, totals, picks = triples[:, 0], triples[:, 1], triples[:, 2]
+    triple = score(wanted_b, token_b, vocab_all, found_a)
+    triples = exchange(triple, SEQ)
+    triples = triples.reshape(BLOCKS, half, 128)[:, :, :6].reshape(BLOCKS, half, 2, 3)
+    tops, totals, picks = triples[..., 0], triples[..., 1], triples[..., 2]
     best = jnp.max(tops, axis=0)
     whole = jnp.sum(totals * jnp.exp(tops - best[None]), axis=0)
     logprob = jnp.sum(picks, axis=0) - best - jnp.log(whole)
-    return (hidden_out, logprob)
+    return (hidden_out, logprob.T.reshape(rows))
 
 
 def solution(mesh):

time: 213 us -> 277 us (1.30)
  waiting for transfers between devices: 41.5 us -> 112 us
  starting transfers between devices: 12.1 us -> 8.63 us
  blocking collectives: 98.8 us -> 102 us
    all_gather x1, waiting for transfers between devices: 0.01 us -> 85.4 us  [inner(): vocab_all = lax.all_gather(vocab, HEAD, axis=0, tiled=True)]
    all_to_all x3 -> x2, waiting for transfers between devices: 40.8 us -> 14.9 us  [exchange(): return lax.all_to_all(value, axes, split_axis=0, concat_axis=0, tiled=True)]
    all_gather x1, waiting for transfers between devices: 0.02 us -> 11.1 us  [inner(): token_a = lax.all_gather(near_a, 'z', axis=0, tiled=True)]
    all_to_all x3 -> x2, starting transfers between devices: 12.1 us -> 8.55 us  [exchange(): return lax.all_to_all(value, axes, split_axis=0, concat_axis=0, tiled=True)]
    all_to_all x4 -> x6, blocking collectives: 98.8 us -> 102 us  [exchange(): return lax.all_to_all(value, axes, split_axis=0, concat_axis=0, tiled=True)]
  transfers between devices with their start and end apart: 5 -> 4, of which waited for: 3 -> 3; matrix products, arithmetic and copies ran while one was open for 8% -> 1% of each run, Pallas kernels for 6% -> 3%
where the time goes in v2:
time: 277 us
  waiting for transfers between devices  112 us (40%)
  blocking collectives  102 us (37%)
  Pallas kernels  21.2 us (8%)
  between operations  14.4 us (5%)
  starting transfers between devices  8.63 us (3%)
  matrix products  7.83 us (3%)
  other arithmetic  6.11 us (2%)
  local copies, waits for them, and re-layouts  4.75 us (2%)
    all_to_all x6, blocking collectives, exchange(): return lax.all_to_all(value, axes, split_axis=0, concat_axis=0, tiled=True)  102 us
    all_gather x1, waiting for transfers between devices, inner(): vocab_all = lax.all_gather(vocab, HEAD, axis=0, tiled=True)  85.4 us
    pallas_call x2, Pallas kernels, score(): pl.pallas_call(score_kernel, grid=(entries // TILE,), in_specs=[pl.BlockS...  18.5 us
    all_to_all x2, waiting for transfers between devices, exchange(): return lax.all_to_all(value, axes, split_axis=0, concat_axis=0, tiled=True)  14.9 us
    all_gather x1, waiting for transfers between devices, inner(): token_a = lax.all_gather(near_a, 'z', axis=0, tiled=True)  11.1 us
    all_to_all x2, starting transfers between devices, exchange(): return lax.all_to_all(value, axes, split_axis=0, concat_axis=0, tiled=True)  8.55 us
  transfers between devices with their start and end apart: 4, of which 3 were waited for; matrix products, arithmetic and copies ran while one was open for 1% of the time, Pallas kernels for 3%

profile of v2, /device:TPU:2, one launch (start us, length us, event | category | flops | bytes accessed | tf_op | source)
XLA Modules:
  0.0 276.5 jit_solution(17038586906682924473)
XLA Ops:
  7.2 0.0 copy-start
  7.2 0.8 copy.41
  8.0 0.2 reduce_window_sum.11
  8.2 0.8 copy.47
  9.0 0.1 copy.48
  9.1 1.1 copy.44
  10.3 0.0 copy-done
  10.3 0.6 fusion.1
  11.0 0.1 pad_maximum_fusion.1
  11.1 30.3 %all_to_all.77 = f16[32,8,1152]{2,1,0:T(8,128)(2,1)S(1)} all-to-all(f16[32,8,1152]{2,1,0:T(8,128)(2,1)S(1)} %pad_maximum_fusion.1), channel_id=1, replica_groups=mesh['z'=8,'y'=4,'x'=4,'core'=2] {'z','y'}, dimensions={0} | all-to-all | bytes 1179648 | tf_op jit(solution)/shard_map/all_to_all | solution.py:133
  41.4 1.1 bitcast_convert_fusion.recv_ref
  42.5 2.7 scan_states.1
  45.2 2.1 convert_bitcast_fusion
  47.3 4.8 %all-to-all-start.1 = ((f16[32,8,1024]{2,1,0:T(8,128)(2,1)}), f16[32,8,1024]{2,1,0:T(8,128)(2,1)S(1)}, u32[]{:S(2)}, u32[]{:S(2)}) async-start(f16[32,8,1024]{2,1,0:T(8,128)(2,1)} %convert_bitcast_fusion), calls=%async_computation.1 | async-start | bytes 1048576 | tf_op jit(solution)/shard_map/all_to_all | solution.py:133
  52.1 0.0 all-gather.5.cloned.1.call-start
  52.2 0.0 copy-done.9
  52.2 0.1 broadcast_in_dim.19
  52.3 0.1 mul.119
  52.4 0.1 copy.46
  52.5 0.0 copy-done.2
  52.5 0.2 copy.49
  52.7 0.0 copy-done.5
  52.7 0.1 fusion.43
  52.8 0.0 copy-done.7
  52.9 1.4 fusion.7
  54.3 14.9 %all-to-all-done.1 = f16[32,8,1024]{2,1,0:T(8,128)(2,1)S(1)} async-done(((f16[32,8,1024]{2,1,0:T(8,128)(2,1)}), f16[32,8,1024]{2,1,0:T(8,128)(2,1)S(1)}, u32[]{:S(2)}, u32[]{:S(2)}) %all-to-all-start.1) | async-done | bytes 524320 | tf_op jit(solution)/shard_map/all_to_all | solution.py:133
  69.2 0.9 multiply_reduce_fusion
  70.1 0.0 copy-done.4
  70.1 4.8 %fusion = f16[128,4096]{1,0:T(8,128)(2,1)S(1)} fusion(bf16[1024,4096]{1,0:T(8,128)(2,1)} %param.21, f32[128,1024]{0,1:T(8,128)S(1)} %get-tuple-element.17, f32[1024]{0:T(1024)S(1)} %copy-done.4, f32[128]{0:T(128)S(1)} %add_rsqrt_fusion.1), kind=kOutput, calls=%fused_computation.1 | convolution fusion | flops 1075183616 | bytes 9966080 | tf_op jit(solution)/shard_map/dot_general | solution.py:189
  74.9 0.2 copy.50
  75.1 4.6 %all_to_all.78 = f16[2,64,4096]{2,1,0:T(8,128)(2,1)S(1)} all-to-all(f16[2,64,4096]{2,1,0:T(8,128)(2,1)S(1)} %bitcast.74), channel_id=1, replica_groups=mesh['z'=8,'y'=4,'x'=4,'core'=2] {'core'}, dimensions={0} | all-to-all | bytes 2097152 | tf_op jit(solution)/shard_map/all_to_all | solution.py:133
  79.6 0.1 convert_element_type.75
  79.8 0.0 copy-start.3
  79.8 0.0 copy-start.6
  79.8 0.1 fusion.6
  80.0 12.9 %all_to_all.79 = f16[4,16,4096]{2,1,0:T(8,128)(2,1)S(1)} all-to-all(f16[4,16,4096]{2,1,0:T(8,128)(2,1)S(1)} %bitcast.75), channel_id=1, replica_groups=mesh['z'=8,'y'=4,'x'=4,'core'=2] {'x'}, dimensions={0} | all-to-all | bytes 1048576 | tf_op jit(solution)/shard_map/all_to_all | solution.py:133
  92.9 0.1 convert_reduce_fusion
  93.0 0.0 copy-done.3
  93.0 0.2 multiply_reduce_fusion.1
  93.2 0.0 copy-done.6
  93.2 0.1 multiply_convert_fusion.2
  93.3 10.1 %all_to_all.80 = bf16[4,8,4096]{2,1,0:T(8,128)(2,1)} all-to-all(bf16[4,8,4096]{2,1,0:T(8,128)(2,1)S(1)} %maximum_bitcast_fusion), channel_id=1, replica_groups=mesh['z'=8,'y'=4,'x'=4,'core'=2] {'y'}, dimensions={0} | all-to-all | bytes 524288 | tf_op jit(solution)/shard_map/all_to_all | solution.py:133
  103.5 0.0 all-gather.5.cloned.1.call-update
  103.5 0.0 all-gather.3.cloned.1.call-start
  103.5 0.7 all-gather.3.cloned.1.call-update
  104.3 0.0 copy-done.1
  104.3 23.2 %all_to_all.81 = bf16[8,8,4096]{2,1,0:T(8,128)(2,1)S(1)} all-to-all(bf16[8,8,4096]{2,1,0:T(8,128)(2,1)S(1)} %bitcast.80), channel_id=1, replica_groups=mesh['z'=8,'y'=4,'x'=4,'core'=2] {'z'}, dimensions={0} | all-to-all | bytes 1048576 | tf_op jit(solution)/shard_map/all_to_all | solution.py:133
  127.5 1.6 pad_maximum_fusion
  129.1 3.7 %all-to-all-start.5 = ((bf16[4,64,4096]{2,1,0:T(8,128)(2,1)}), bf16[4,64,4096]{2,1,0:T(8,128)(2,1)S(1)}, u32[]{:S(2)}, u32[]{:S(2)}) async-start(bf16[4,64,4096]{2,1,0:T(8,128)(2,1)} %bitcast.72), calls=%async_computation.5 | async-start | bytes 4194304 | tf_op jit(solution)/shard_map/all_to_all | solution.py:133
  132.9 0.0 copy-done.8
  132.9 0.1 copy.51
  133.0 0.1 fusion.42
  133.0 0.1 reshape.119.refs_0_
  133.1 0.1 reshape.118.refs_0_
  133.2 11.1 %all-gather.5.cloned.1.call-done.refs_1_ = bf16[256,4096]{1,0:T(8,128)(2,1)} async-done(((bf16[32,4096]{1,0:T(8,128)(2,1)}), bf16[256,4096]{1,0:T(8,128)(2,1)}) %all-gather.5.cloned.1.call-update) | async-done | bytes 2097168 | tf_op jit(solution)/shard_map/all_gather | solution.py:206
  144.3 85.4 %all-gather.3.cloned.1.call-done.refs_2_ = bf16[2048,4096]{1,0:T(8,128)(2,1)} async-done(((bf16[256,4096]{1,0:T(8,128)(2,1)}), bf16[2048,4096]{1,0:T(8,128)(2,1)}) %all-gather.3.cloned.1.call-update) | async-done | bytes 16777232 | tf_op jit(solution)/shard_map/all_gather | solution.py:153
  229.7 9.6 %score.2.refs_3_ = f32[256,128]{1,0:T(8,128)S(1)} custom-call(s32[1,256]{1,0:T(1,128)S(1)} %reshape.119.refs_0_, bf16[256,4096]{1,0:T(8,128)(2,1)} %all-gather.5.cloned.1.call-done.refs_1_, bf16[2048,4096]{1,0:T(8,128)(2,1)} %all-gather.3.cloned.1.call-done.refs_2_), custom_call_target="tpu_custom_call" | custom-call | flops 4294967296 | bytes 18874368 | tf_op jit(solution)/shard_map/score/pallas_call | solution.py:110
  239.2 0.0 all-to-all-done.5
  239.3 8.9 %score.3 = f32[256,128]{1,0:T(8,128)S(1)} custom-call(s32[1,256]{1,0:T(1,128)S(1)} %reshape.118.refs_0_, bf16[256,4096]{1,0:T(8,128)(2,1)S(1)} %bitcast.70, bf16[2048,4096]{1,0:T(8,128)(2,1)} %all-gather.3.cloned.1.call-done.refs_2_, f32[256,128]{1,0:T(8,128)S(1)} %score.2.refs_3_), custom_call_target="tpu_custom_call" | custom-call | flops 4294967296 | bytes 18874368 | tf_op jit(solution)/shard_map/score/pallas_call | solution.py:110
  248.2 20.5 %all_to_all.82 = f32[32,8,128]{2,1,0:T(8,128)S(1)} all-to-all(f32[32,8,128]{2,1,0:T(8,128)S(1)} %bitcast.71), channel_id=1, replica_groups=mesh['z'=8,'y'=4,'x'=4,'core'=2] {'z','y'}, dimensions={0} | all-to-all | bytes 262144 | tf_op jit(solution)/shard_map/all_to_all | solution.py:133
  268.7 0.1 copy.54
  268.8 0.1 slice_reduce_fusion
  268.9 0.2 fusion.28
  269.1 0.6 reshape.121
  (29 shorter events, 0.3 us)
Async XLA Ops:
  7.2 3.1 %copy-start = (bf16[128,256]{1,0:T(8,128)(2,1)S(1)}, bf16[128,256]{1,0:T(8,128)(2,1)}, u32[]{:S(2)}) copy-start(bf16[128,256]{1,0:T(8,128)(2,1)} %param.15) | copy-start | bytes 196612
  42.5 9.7 %copy-start.9 = (f32[16]{0:T(128)S(1)}, f32[16]{0:T(128)}, u32[]{:S(2)}) copy-start(f32[16]{0:T(128)} %param.19) | copy-start | bytes 196
  42.5 10.0 %copy-start.2 = (bf16[128,1024]{1,0:T(8,128)(2,1)S(1)}, bf16[128,1024]{1,0:T(8,128)(2,1)}, u32[]{:S(2)}) copy-start(bf16[128,1024]{1,0:T(8,128)(2,1)} %param.14) | copy-start | bytes 786436
  45.2 7.5 %copy-start.5 = (bf16[128,256]{1,0:T(8,128)(2,1)S(1)}, bf16[128,256]{1,0:T(8,128)(2,1)}, u32[]{:S(2)}) copy-start(bf16[128,256]{1,0:T(8,128)(2,1)} %param.16) | copy-start | bytes 196612
  45.2 7.7 %copy-start.7 = (f32[128,16]{0,1:T(8,128)S(1)}, f32[128,16]{0,1:T(8,128)}, u32[]{:S(2)}) copy-start(f32[128,16]{0,1:T(8,128)} %param.18) | copy-start | bytes 24580
  47.3 21.8 %all-to-all-start.1 = ((f16[32,8,1024]{2,1,0:T(8,128)(2,1)}), f16[32,8,1024]{2,1,0:T(8,128)(2,1)S(1)}, u32[]{:S(2)}, u32[]{:S(2)}) async-start(f16[32,8,1024]{2,1,0:T(8,128)(2,1)} %convert_bitcast_fusion), calls=%async_computation.1 | async-start | bytes 1048576 | tf_op jit(solution)/shard_map/all_to_all | solution.py:133
  52.1 92.1 %all-gather.5.cloned.1.call-start = ((), (), s32[]{:S(2)}) async-start(), calls=%async_computation.9 | async-start | bytes 2359296 | tf_op jit(solution)/shard_map/all_gather | solution.py:206
  69.1 1.0 copy-start.4
  79.8 13.2 %copy-start.3 = (bf16[16,4096]{1,0:T(8,128)(2,1)S(1)}, bf16[16,4096]{1,0:T(8,128)(2,1)}, u32[]{:S(2)}) copy-start(bf16[16,4096]{1,0:T(8,128)(2,1)} %param.22) | copy-start | bytes 393220
  79.8 13.4 %copy-start.6 = (f32[4096]{0:T(1024)S(1)}, f32[4096]{0:T(1024)}, u32[]{:S(2)}) copy-start(f32[4096]{0:T(1024)} %param.23) | copy-start | bytes 49156
  93.1 11.1 %copy-start.1 = (f32[16,4096]{1,0:T(8,128)}, f32[16,4096]{1,0:T(8,128)S(1)}, u32[]{:S(2)}) copy-start(f32[16,4096]{1,0:T(8,128)S(1)} %get-tuple-element.5) | copy-start | bytes 786436
  103.5 126.2 %all-gather.3.cloned.1.call-start = ((), (), s32[]{:S(2)}) async-start(), calls=%async_computation.8 | async-start | bytes 18874368 | tf_op jit(solution)/shard_map/all_gather | solution.py:153
  129.1 3.8 %copy-start.8 = (s32[32,16]{0,1:T(8,128)S(1)}, s32[32,16]{0,1:T(8,128)}, u32[]{:S(2)}) copy-start(s32[32,16]{0,1:T(8,128)} %param.25) | copy-start | bytes 6148
  129.1 110.1 %all-to-all-start.5 = ((bf16[4,64,4096]{2,1,0:T(8,128)(2,1)}), bf16[4,64,4096]{2,1,0:T(8,128)(2,1)S(1)}, u32[]{:S(2)}, u32[]{:S(2)}) async-start(bf16[4,64,4096]{2,1,0:T(8,128)(2,1)} %bitcast.72), calls=%async_computation.5 | async-start | bytes 4194304 | tf_op jit(solution)/shard_map/all_to_all | solution.py:133
Sparse Core Ops, SparseCore 0:
  103.6 40.6 all-gather.4
  146.1 83.4 all-gather.2

commit v3 on v2

--- a/solution.py
+++ b/solution.py
@@ -14,6 +14,7 @@
 HALF = jnp.float16
 PART_SCALE = 512.0
 TILE = 512
+SPAN = 2048
 
 epsilon = 1e-05
 highest = lax.Precision.HIGHEST
@@ -73,7 +74,7 @@
         (((1,), (1,)), ((), ())),
         preferred_element_type=jnp.float32,
     )
-    ids = step * TILE + lax.broadcasted_iota(jnp.int32, logits.shape, 0)
+    ids = step * SPAN + lax.broadcasted_iota(jnp.int32, logits.shape, 0)
     hit = jnp.where(ids == wanted_ref[...], logits, 0.0)
     hit_ref[...] += jnp.sum(hit.reshape(TILE // 8, 8, count), axis=0)
     folded = logits.reshape(TILE // 8, 8, count)
@@ -93,15 +94,13 @@
         row = lax.broadcasted_iota(jnp.int32, (128, count), 0) % 3
         packed = jnp.where(row == 0, top, jnp.where(row == 1, total, picked)).T
         if near_ref is None:
-            out_ref[...] = packed
+            for z in range(8):
+                for x in range(4):
+                    here = (x * 8 + z) * 8
+                    out_ref[pl.ds((z * 4 + x) * 8, 8), :] = packed[here : here + 8]
         else:
-            lane = lax.broadcasted_iota(jnp.int32, (8, 128), 1)
-            for z in range(8):
-                for y in range(4):
-                    there = pl.ds((z * 4 + y) * 8, 8)
-                    here = (y * 8 + z) * 8
-                    far = packed[here : here + 8]
-                    out_ref[there, :] = jnp.where(lane < 3, near_ref[there, :], far)
+            lane = lax.broadcasted_iota(jnp.int32, packed.shape, 1)
+            out_ref[...] = jnp.where(lane < 3, packed, near_ref[...])
 
 
 def score(wanted, token, vocab, *near):
@@ -124,7 +123,7 @@
             bytes_accessed=2 * (count + entries) * width,
             transcendentals=count * entries,
         ),
-        compiler_params=pltpu.CompilerParams(vmem_limit_bytes=(48 if near else 52) * 2**20),
+        compiler_params=pltpu.CompilerParams(vmem_limit_bytes=(52 if near else 48) * 2**20),
         name="score",
     )(wanted, token, vocab, *near)
 
@@ -150,7 +149,7 @@
 ):
     length = x_in.shape[0]
     heads = log_decay.shape[1]
-    vocab_all = lax.all_gather(vocab, HEAD, axis=0, tiled=True)
+    vocab_all = lax.all_gather(vocab, ("y", "core"), axis=0, tiled=True)
 
     inputs = x_in.astype(jnp.float32)
     cumulative = jnp.cumsum(log_decay, axis=0)
@@ -191,9 +190,16 @@
     swapped = (partial * PART_SCALE).astype(HALF).reshape(4, 2, rows, -1).transpose(1, 0, 2, 3)
     pair = exchange(swapped.reshape(length, -1), "core")
     pair = pair.reshape(2, length // 2, -1).astype(jnp.float32)
-    pair = ((pair[0] + pair[1]) * 0.5).astype(HALF)
-    parts = exchange(pair, "x")
-    summed = jnp.sum(parts.reshape(4, rows, -1).astype(jnp.float32), axis=0) * (2.0 / PART_SCALE)
+    pair = ((pair[0] + pair[1]) * 0.5).astype(HALF).reshape(4, rows, -1)
+    width = pair.shape[-1]
+    ids = lax.dynamic_index_in_dim(targets.reshape(8, 4, rows), lax.axis_index("y"), 1, False)
+    side = jnp.concatenate([ids // 256, ids % 256], axis=0).astype(HALF)
+    side = jnp.broadcast_to(jnp.pad(side, ((0, 0), (0, EXTRA - rows)))[None], (4, rows, EXTRA))
+    pair = jnp.concatenate([pair, side], axis=-1).reshape(length // 2, width + EXTRA)
+    parts = exchange(pair, "x").reshape(4, rows, width + EXTRA).astype(jnp.float32)
+    summed = jnp.sum(parts[:, :, :width], axis=0) * (2.0 / PART_SCALE)
+    ids = parts[:, :, width : width + rows].astype(jnp.int32)
+    ids = ids[:, :8] * 256 + ids[:, 8:]
     hidden_out = residual.astype(jnp.float32) + summed
     normed = (
         hidden_out
@@ -202,18 +208,17 @@
     ).astype(jnp.bfloat16)
 
     half = rows // 2
-    near_a = exchange(jnp.concatenate([normed[:half]] * 4, axis=0), "y")
+    near_a = exchange(jnp.concatenate([normed[:half]] * 4, axis=0), "x")
     token_a = lax.all_gather(near_a, "z", axis=0, tiled=True)
     far_b = exchange(jnp.concatenate([normed[half:]] * 8, axis=0), "z")
-    token_b = exchange(jnp.concatenate([far_b] * 4, axis=0), "y")
-
-    offset = lax.axis_index(SEQ) * vocab_all.shape[0]
-    wanted = (targets - offset).reshape(8, 4, rows)
-    wanted_a = wanted[:, :, :half].reshape(1, -1)
-    wanted_b = wanted[:, :, half:].transpose(1, 0, 2).reshape(1, -1)
-    found_a = score(wanted_a, token_a, vocab_all)
-    triple = score(wanted_b, token_b, vocab_all, found_a)
-    triples = exchange(triple, SEQ)
+    token_b = exchange(jnp.concatenate([far_b] * 4, axis=0), "x")
+
+    ids = ids - (lax.axis_index("z") * (4 * SPAN) + lax.axis_index("x") * TILE)
+    wanted_a = ids[:, :, :half].transpose(1, 0, 2).reshape(1, -1)
+    wanted_b = ids[:, :, half:].reshape(1, -1)
+    found_b = score(wanted_b, token_b, vocab_all)
+    triple = score(wanted_a, token_a, vocab_all, found_b)
+    triples = exchange(triple, ("z", "x"))
     triples = triples.reshape(BLOCKS, half, 128)[:, :, :6].reshape(BLOCKS, half, 2, 3)
     tops, totals, picks = triples[..., 0], triples[..., 1], triples[..., 2]
     best = jnp.max(tops, axis=0)

time: 277 us -> 192 us (0.69)
  waiting for transfers between devices: 112 us -> 55.8 us
  blocking collectives: 102 us -> 61.1 us
  starting transfers between devices: 8.63 us -> 21 us
    all_gather x1, waiting for transfers between devices: 85.4 us -> 0.01 us  [inner(): vocab_all = lax.all_gather(vocab, ('y', 'core'), axis=0, tiled=True)]
    all_to_all x6 -> x5, blocking collectives: 102 us -> 61.1 us  [exchange(): return lax.all_to_all(value, axes, split_axis=0, concat_axis=0, tiled=True)]
    all_to_all x2 -> x3, waiting for transfers between devices: 14.9 us -> 55.1 us  [exchange(): return lax.all_to_all(value, axes, split_axis=0, concat_axis=0, tiled=True)]
    all_to_all x2 -> x3, starting transfers between devices: 8.55 us -> 21 us  [exchange(): return lax.all_to_all(value, axes, split_axis=0, concat_axis=0, tiled=True)]
    all_gather x1, waiting for transfers between devices: 11.1 us -> 0.02 us  [inner(): token_a = lax.all_gather(near_a, 'z', axis=0, tiled=True)]
  transfers between devices with their start and end apart: 4 -> 5, of which waited for: 3 -> 3; matrix products, arithmetic and copies ran while one was open for 1% -> 9% of each run, Pallas kernels for 3% -> 6%
where the time goes in v3:
time: 192 us; the launch traced here: 191 us
  blocking collectives  61.1 us (32%)
  waiting for transfers between devices  55.8 us (29%)
  Pallas kernels  21.2 us (11%)
  starting transfers between devices  21 us (11%)
  between operations  14.5 us (8%)
  matrix products  8.05 us (4%)
  other arithmetic  7.11 us (4%)
  local copies, waits for them, and re-layouts  2.38 us (1%)
    all_to_all x5, blocking collectives, exchange(): return lax.all_to_all(value, axes, split_axis=0, concat_axis=0, tiled=True)  61.1 us
    all_to_all x3, waiting for transfers between devices, exchange(): return lax.all_to_all(value, axes, split_axis=0, concat_axis=0, tiled=True)  55.1 us
    all_to_all x3, starting transfers between devices, exchange(): return lax.all_to_all(value, axes, split_axis=0, concat_axis=0, tiled=True)  21 us
    pallas_call x2, Pallas kernels, score(): pl.pallas_call(score_kernel, grid=(entries // TILE,), in_specs=[pl.BlockS...  18.5 us
    dot_general x1, matrix products, inner(): partial = jnp.dot(normed_inner, w_out, preferred_element_type=jnp.float32)  4.98 us
  transfers between devices with their start and end apart: 5, of which 3 were waited for; matrix products, arithmetic and copies ran while one was open for 9% of the time, Pallas kernels for 6%

profile of v3, /device:TPU:2, one launch (start us, length us, event | category | flops | bytes accessed | tf_op | source)
XLA Modules:
  0.0 191.1 jit_solution(5766279031315168803)
XLA Ops:
  7.2 0.0 copy-start
  7.2 0.0 copy-start.8
  7.2 0.0 copy-start.10
  7.2 0.0 copy-start.2
  7.2 0.0 all-gather.5.cloned.1.call-start
  7.3 0.7 all-gather.5.cloned.1.call-update
  8.0 0.1 copy.40
  8.1 0.0 copy-done.10
  8.1 0.1 copy.46
  8.2 0.2 reduce_window_sum.11
  8.4 0.1 copy.47
  8.5 0.2 copy.43
  8.7 0.0 copy-start.3
  8.7 0.0 copy-start.11
  8.7 0.0 copy-start.9
  8.8 0.6 fusion.1
  9.4 1.0 pad_maximum_fusion.1
  10.4 11.5 %all-to-all-start = ((f16[32,8,1152]{2,1,0:T(8,128)(2,1)}), f16[32,8,1152]{2,1,0:T(8,128)(2,1)S(1)}, u32[]{:S(2)}, u32[]{:S(2)}) async-start(f16[32,8,1152]{2,1,0:T(8,128)(2,1)} %pad_maximum_fusion.1), calls=%async_computation | async-start | bytes 1179648 | tf_op jit(solution)/shard_map/all_to_all | solution.py:132
  21.9 0.1 copy.45
  21.9 0.1 copy.41
  22.0 0.2 copy.48
  22.2 0.1 broadcast_in_dim.21
  22.3 0.1 mul.127
  22.3 0.1 copy.50
  22.4 18.5 %all-to-all-done = f16[32,8,1152]{2,1,0:T(8,128)(2,1)S(1)} async-done(((f16[32,8,1152]{2,1,0:T(8,128)(2,1)}), f16[32,8,1152]{2,1,0:T(8,128)(2,1)S(1)}, u32[]{:S(2)}, u32[]{:S(2)}) %all-to-all-start) | async-done | bytes 589856 | tf_op jit(solution)/shard_map/all_to_all | solution.py:132
  41.0 1.1 bitcast_convert_fusion.recv_ref
  42.1 2.7 %scan_states.1 = f32[256,1024]{1,0:T(8,128)} custom-call(f32[256,1152]{1,0:T(8,128)} %bitcast_convert_fusion.recv_ref), custom_call_target="tpu_custom_call" | custom-call | tf_op jit(solution)/shard_map/scan_states/pallas_call | solution.py:51
  44.8 2.1 %convert_bitcast_fusion = f16[32,8,1024]{2,1,0:T(8,128)(2,1)} fusion(f32[256,1024]{1,0:T(8,128)} %scan_states.1), kind=kLoop, calls=%fused_computation.34 | loop fusion | flops 262144 | bytes 1572864 | tf_op jit(solution)/shard_map/all_to_all | solution.py:132
  46.9 4.7 %all-to-all-start.1 = ((f16[32,8,1024]{2,1,0:T(8,128)(2,1)}), f16[32,8,1024]{2,1,0:T(8,128)(2,1)S(1)}, u32[]{:S(2)}, u32[]{:S(2)}) async-start(f16[32,8,1024]{2,1,0:T(8,128)(2,1)} %convert_bitcast_fusion), calls=%async_computation.1 | async-start | bytes 1048576 | tf_op jit(solution)/shard_map/all_to_all | solution.py:132
  51.6 0.0 all-gather.3.cloned.1.call-start
  51.7 0.1 fusion.50
  51.9 1.4 fusion.7
  53.3 0.0 copy-start.5
  53.3 15.2 %all-to-all-done.1 = f16[32,8,1024]{2,1,0:T(8,128)(2,1)S(1)} async-done(((f16[32,8,1024]{2,1,0:T(8,128)(2,1)}), f16[32,8,1024]{2,1,0:T(8,128)(2,1)S(1)}, u32[]{:S(2)}, u32[]{:S(2)}) %all-to-all-start.1) | async-done | bytes 524320 | tf_op jit(solution)/shard_map/all_to_all | solution.py:132
  68.6 0.9 multiply_reduce_fusion
  69.5 5.0 %fusion = f16[128,4096]{1,0:T(8,128)(2,1)S(1)} fusion(bf16[1024,4096]{1,0:T(8,128)(2,1)} %param.21, f32[128,1024]{0,1:T(8,128)S(1)} %get-tuple-element.19, f32[1024]{0:T(1024)S(1)} %copy-done.5, f32[128]{0:T(128)S(1)} %add_rsqrt_fusion.1), kind=kOutput, calls=%fused_computation.1 | convolution fusion | flops 1075183616 | bytes 9966080 | tf_op jit(solution)/shard_map/dot_general | solution.py:188
  74.5 0.2 copy.49
  74.7 4.6 %all_to_all.77 = f16[2,64,4096]{2,1,0:T(8,128)(2,1)S(1)} all-to-all(f16[2,64,4096]{2,1,0:T(8,128)(2,1)S(1)} %bitcast.75), channel_id=1, replica_groups=mesh['z'=8,'y'=4,'x'=4,'core'=2] {'core'}, dimensions={0} | all-to-all | bytes 2097152 | tf_op jit(solution)/shard_map/all_to_all | solution.py:132
  79.3 0.1 convert_element_type.83
  79.4 0.1 fusion.6
  79.6 0.1 pad_maximum_fusion.2
  79.7 0.0 copy-start.4
  79.7 0.0 copy-start.7
  79.7 13.3 %all_to_all.78 = f16[4,16,4224]{2,1,0:T(8,128)(2,1)S(1)} all-to-all(f16[4,16,4224]{2,1,0:T(8,128)(2,1)S(1)} %pad_maximum_fusion.2), channel_id=1, replica_groups=mesh['z'=8,'y'=4,'x'=4,'core'=2] {'x'}, dimensions={0} | all-to-all | bytes 1081344 | tf_op jit(solution)/shard_map/all_to_all | solution.py:132
  93.0 0.1 convert_element_type.86
  93.1 0.2 multiply_reduce_fusion.1
  93.3 0.1 multiply_convert_fusion.2
  93.6 9.7 %all_to_all.79 = bf16[4,8,4096]{2,1,0:T(8,128)(2,1)} all-to-all(bf16[4,8,4096]{2,1,0:T(8,128)(2,1)S(1)} %maximum_bitcast_fusion), channel_id=1, replica_groups=mesh['z'=8,'y'=4,'x'=4,'core'=2] {'x'}, dimensions={0} | all-to-all | bytes 524288 | tf_op jit(solution)/shard_map/all_to_all | solution.py:132
  103.3 0.0 all-gather.3.cloned.1.call-update
  103.3 18.8 %all_to_all.80 = bf16[8,8,4096]{2,1,0:T(8,128)(2,1)S(1)} all-to-all(bf16[8,8,4096]{2,1,0:T(8,128)(2,1)S(1)} %bitcast.81), channel_id=1, replica_groups=mesh['z'=8,'y'=4,'x'=4,'core'=2] {'z'}, dimensions={0} | all-to-all | bytes 1048576 | tf_op jit(solution)/shard_map/all_to_all | solution.py:132
  122.1 1.6 pad_maximum_fusion
  123.7 4.7 %all-to-all-start.6 = ((bf16[4,64,4096]{2,1,0:T(8,128)(2,1)}), bf16[4,64,4096]{2,1,0:T(8,128)(2,1)S(1)}, u32[]{:S(2)}, u32[]{:S(2)}) async-start(bf16[4,64,4096]{2,1,0:T(8,128)(2,1)} %bitcast.73), calls=%async_computation.6 | async-start | bytes 4194304 | tf_op jit(solution)/shard_map/all_to_all | solution.py:132
  128.5 0.1 fusion.49
  128.5 0.1 reshape.131.refs_0_
  128.6 0.1 reshape.130.refs_0_
  128.7 21.3 %all-to-all-done.6 = bf16[4,64,4096]{2,1,0:T(8,128)(2,1)S(1)} async-done(((bf16[4,64,4096]{2,1,0:T(8,128)(2,1)}), bf16[4,64,4096]{2,1,0:T(8,128)(2,1)S(1)}, u32[]{:S(2)}, u32[]{:S(2)}) %all-to-all-start.6) | async-done | bytes 2097184 | tf_op jit(solution)/shard_map/all_to_all | solution.py:132
  150.0 8.9 %score.2.refs_3_ = f32[256,128]{1,0:T(8,128)S(1)} custom-call(s32[1,256]{1,0:T(1,128)S(1)} %reshape.131.refs_0_, bf16[256,4096]{1,0:T(8,128)(2,1)S(1)} %bitcast.71, bf16[2048,4096]{1,0:T(8,128)(2,1)} %all-gather.5.cloned.1.call-done.refs_2_), custom_call_target="tpu_custom_call" | custom-call | flops 4294967296 | bytes 18874368 | tf_op jit(solution)/shard_map/score/pallas_call | solution.py:109
  158.9 0.0 all-gather.3.cloned.1.call-done.refs_1_
  159.0 9.6 %score.3 = f32[256,128]{1,0:T(8,128)S(1)} custom-call(s32[1,256]{1,0:T(1,128)S(1)} %reshape.130.refs_0_, bf16[256,4096]{1,0:T(8,128)(2,1)} %all-gather.3.cloned.1.call-done.refs_1_, bf16[2048,4096]{1,0:T(8,128)(2,1)} %all-gather.5.cloned.1.call-done.refs_2_, f32[256,128]{1,0:T(8,128)S(1)} %score.2.refs_3_), custom_call_target="tpu_custom_call" | custom-call | flops 4294967296 | bytes 18874368 | tf_op jit(solution)/shard_map/score/pallas_call | solution.py:109
  168.6 14.7 %all_to_all.81 = f32[32,8,128]{2,1,0:T(8,128)S(1)} all-to-all(f32[32,8,128]{2,1,0:T(8,128)S(1)} %bitcast.72), channel_id=1, replica_groups=mesh['z'=8,'y'=4,'x'=4,'core'=2] {'z','x'}, dimensions={0} | all-to-all | bytes 262144 | tf_op jit(solution)/shard_map/all_to_all | solution.py:132
  183.3 0.1 copy.53
  183.4 0.1 slice_reduce_fusion.1
  183.5 0.2 fusion.29
  183.6 0.6 reshape.133
  (41 shorter events, 0.4 us)
Async XLA Ops:
  7.2 1.6 copy-start
  7.2 0.8 copy-start.8
  7.2 0.9 copy-start.10
  7.2 1.2 copy-start.2
  7.2 142.8 %all-gather.5.cloned.1.call-start = ((), (), s32[]{:S(2)}) async-start(), calls=%async_computation.9 | async-start | bytes 18874368 | tf_op jit(solution)/shard_map/all_gather | solution.py:152
  8.7 13.3 %copy-start.3 = (bf16[128,1024]{1,0:T(8,128)(2,1)S(1)}, bf16[128,1024]{1,0:T(8,128)(2,1)}, u32[]{:S(2)}) copy-start(bf16[128,1024]{1,0:T(8,128)(2,1)} %param.14) | copy-start | bytes 786436
  8.7 13.5 %copy-start.11 = (f32[16]{0:T(128)S(1)}, f32[16]{0:T(128)}, u32[]{:S(2)}) copy-start(f32[16]{0:T(128)} %param.19) | copy-start | bytes 196
  8.7 13.6 %copy-start.9 = (s32[32,16]{0,1:T(8,128)S(1)}, s32[32,16]{0,1:T(8,128)}, u32[]{:S(2)}) copy-start(s32[32,16]{0,1:T(8,128)} %param.25) | copy-start | bytes 6148
  10.4 30.6 %all-to-all-start = ((f16[32,8,1152]{2,1,0:T(8,128)(2,1)}), f16[32,8,1152]{2,1,0:T(8,128)(2,1)S(1)}, u32[]{:S(2)}, u32[]{:S(2)}) async-start(f16[32,8,1152]{2,1,0:T(8,128)(2,1)} %pad_maximum_fusion.1), calls=%async_computation | async-start | bytes 1179648 | tf_op jit(solution)/shard_map/all_to_all | solution.py:132
  42.1 9.7 %copy-start.6 = (bf16[128,256]{1,0:T(8,128)(2,1)S(1)}, bf16[128,256]{1,0:T(8,128)(2,1)}, u32[]{:S(2)}) copy-start(bf16[128,256]{1,0:T(8,128)(2,1)} %param.16) | copy-start | bytes 196612
  46.9 21.7 %all-to-all-start.1 = ((f16[32,8,1024]{2,1,0:T(8,128)(2,1)}), f16[32,8,1024]{2,1,0:T(8,128)(2,1)S(1)}, u32[]{:S(2)}, u32[]{:S(2)}) async-start(f16[32,8,1024]{2,1,0:T(8,128)(2,1)} %convert_bitcast_fusion), calls=%async_computation.1 | async-start | bytes 1048576 | tf_op jit(solution)/shard_map/all_to_all | solution.py:132
  51.6 107.4 %all-gather.3.cloned.1.call-start = ((), (), s32[]{:S(2)}) async-start(), calls=%async_computation.8 | async-start | bytes 2359296 | tf_op jit(solution)/shard_map/all_gather | solution.py:212
  53.3 16.2 %copy-start.5 = (f32[1024]{0:T(1024)S(1)}, f32[1024]{0:T(1024)}, u32[]{:S(2)}) copy-start(f32[1024]{0:T(1024)} %param.20) | copy-start | bytes 12292
  79.7 13.4 %copy-start.4 = (bf16[16,4096]{1,0:T(8,128)(2,1)S(1)}, bf16[16,4096]{1,0:T(8,128)(2,1)}, u32[]{:S(2)}) copy-start(bf16[16,4096]{1,0:T(8,128)(2,1)} %param.22) | copy-start | bytes 393220
  79.7 13.6 %copy-start.7 = (f32[4096]{0:T(1024)S(1)}, f32[4096]{0:T(1024)}, u32[]{:S(2)}) copy-start(f32[4096]{0:T(1024)} %param.23) | copy-start | bytes 49156
  93.3 30.4 %copy-start.1 = (f32[16,4096]{1,0:T(8,128)}, f32[16,4096]{1,0:T(8,128)S(1)}, u32[]{:S(2)}) copy-start(f32[16,4096]{1,0:T(8,128)S(1)} %get-tuple-element.5) | copy-start | bytes 786436
  123.7 26.3 %all-to-all-start.6 = ((bf16[4,64,4096]{2,1,0:T(8,128)(2,1)}), bf16[4,64,4096]{2,1,0:T(8,128)(2,1)S(1)}, u32[]{:S(2)}, u32[]{:S(2)}) async-start(bf16[4,64,4096]{2,1,0:T(8,128)(2,1)} %bitcast.73), calls=%async_computation.6 | async-start | bytes 4194304 | tf_op jit(solution)/shard_map/all_to_all | solution.py:132
Sparse Core Ops, SparseCore 0:
  9.9 100.2 all-gather.4
  111.9 39.7 all-gather.2

commit v4 on v3

--- a/solution.py
+++ b/solution.py
@@ -1,3 +1,5 @@
+import functools
+
 import jax
 import jax.numpy as jnp
 from jax import lax
@@ -55,18 +57,26 @@
     )(received.astype(jnp.float32)).astype(HALF)
 
 
-def score_kernel(*refs):
-    wanted_ref, token_ref, vocab_ref = refs[:3]
-    near_ref = refs[3] if len(refs) == 8 else None
-    out_ref, top_ref, total_ref, hit_ref = refs[-4:]
+def score_kernel(*refs, count, parts):
+    here_ref, wanted_ref, vocab_ref = refs[:3]
+    token_refs = refs[3 : 3 + parts]
+    if parts == 1:
+        near_ref, out_ref, top_ref, total_ref, hit_ref = refs[4:]
+        token_ref = token_refs[0]
+    else:
+        out_ref, top_ref, total_ref, hit_ref, token_ref = refs[3 + parts :]
     step = pl.program_id(0)
-    count = token_ref.shape[0]
 
     @pl.when(step == 0)
     def _():
         top_ref[...] = jnp.full(top_ref.shape, -jnp.inf, jnp.float32)
         total_ref[...] = jnp.zeros(total_ref.shape, jnp.float32)
         hit_ref[...] = jnp.zeros(hit_ref.shape, jnp.float32)
+        if parts > 1:
+            at = 0
+            for part_ref in token_refs:
+                token_ref[at : at + part_ref.shape[0], :] = part_ref[...]
+                at += part_ref.shape[0]
 
     logits = lax.dot_general(
         vocab_ref[...],
@@ -93,31 +103,35 @@
         picked = jnp.sum(hit_ref[...], axis=0, keepdims=True)
         row = lax.broadcasted_iota(jnp.int32, (128, count), 0) % 3
         packed = jnp.where(row == 0, top, jnp.where(row == 1, total, picked)).T
-        if near_ref is None:
-            for z in range(8):
-                for x in range(4):
-                    here = (x * 8 + z) * 8
-                    out_ref[pl.ds((z * 4 + x) * 8, 8), :] = packed[here : here + 8]
+        if parts > 1:
+            out_ref[...] = packed
         else:
-            lane = lax.broadcasted_iota(jnp.int32, packed.shape, 1)
-            out_ref[...] = jnp.where(lane < 3, packed, near_ref[...])
-
-
-def score(wanted, token, vocab, *near):
-    count, width = token.shape
-    entries = vocab.shape[0]
+            lane = lax.broadcasted_iota(jnp.int32, (8, 128), 1)
+            for x in range(4):
+                part = lax.rem(here_ref[0] + (4 - x), 4)
+                for z in range(8):
+                    at = (z * 4 + x) * 8
+                    near = near_ref[pl.ds(pl.multiple_of(part * 64 + z * 8, 8), 8), :]
+                    out_ref[pl.ds(at, 8), :] = jnp.where(lane < 3, packed[at : at + 8], near)
+
+
+def score(here, wanted, tokens, vocab, *near):
+    count = sum(token.shape[0] for token in tokens)
+    entries, width = vocab.shape
+    stats = [pltpu.VMEM((8, count), jnp.float32)] * 3
     return pl.pallas_call(
-        score_kernel,
+        functools.partial(score_kernel, count=count, parts=len(tokens)),
         grid=(entries // TILE,),
         in_specs=[
+            pl.BlockSpec(memory_space=pltpu.SMEM),
             pl.BlockSpec((1, count), lambda i: (0, 0)),
-            pl.BlockSpec((count, width), lambda i: (0, 0)),
             pl.BlockSpec((TILE, width), lambda i: (i, 0)),
         ]
+        + [pl.BlockSpec(token.shape, lambda i: (0, 0)) for token in tokens]
         + [pl.BlockSpec((count, 128), lambda i: (0, 0))] * len(near),
         out_specs=pl.BlockSpec((count, 128), lambda i: (0, 0)),
         out_shape=jax.ShapeDtypeStruct((count, 128), jnp.float32),
-        scratch_shapes=[pltpu.VMEM((8, count), jnp.float32)] * 3,
+        scratch_shapes=stats + [pltpu.VMEM((count, width), vocab.dtype)] * (len(tokens) > 1),
         cost_estimate=pl.CostEstimate(
             flops=2 * count * width * entries,
             bytes_accessed=2 * (count + entries) * width,
@@ -125,7 +139,11 @@
         ),
         compiler_params=pltpu.CompilerParams(vmem_limit_bytes=(52 if near else 48) * 2**20),
         name="score",
-    )(wanted, token, vocab, *near)
+    )(here.reshape(1), wanted, vocab, *tokens, *near)
+
+
+def copies(value, count):
+    return jnp.broadcast_to(value[None], (count,) + value.shape).reshape(-1, value.shape[1])
 
 
 def exchange(value, axes):
@@ -208,16 +226,24 @@
     ).astype(jnp.bfloat16)
 
     half = rows // 2
-    near_a = exchange(jnp.concatenate([normed[:half]] * 4, axis=0), "x")
+    near_a = exchange(copies(normed[:half], 4), "x")
     token_a = lax.all_gather(near_a, "z", axis=0, tiled=True)
-    far_b = exchange(jnp.concatenate([normed[half:]] * 8, axis=0), "z")
-    token_b = exchange(jnp.concatenate([far_b] * 4, axis=0), "x")
+    far_b = exchange(copies(normed[half:], 8), "z")
+    up = [(i, (i + 1) % 4) for i in range(4)]
+    down = [(i, (i - 1) % 4) for i in range(4)]
+    quarter = far_b.shape[0] // 2
+    one_up = lax.ppermute(far_b, "x", up)
+    one_down = lax.ppermute(far_b, "x", down)
+    two_up = lax.ppermute(one_up[:quarter], "x", up)
+    two_down = lax.ppermute(one_down[quarter:], "x", down)
+    token_b = (far_b, one_up, two_up, two_down, one_down)
 
     ids = ids - (lax.axis_index("z") * (4 * SPAN) + lax.axis_index("x") * TILE)
     wanted_a = ids[:, :, :half].transpose(1, 0, 2).reshape(1, -1)
-    wanted_b = ids[:, :, half:].reshape(1, -1)
-    found_b = score(wanted_b, token_b, vocab_all)
-    triple = score(wanted_a, token_a, vocab_all, found_b)
+    here = lax.axis_index("x")
+    wanted_b = jnp.take(ids, (here - jnp.arange(4)) % 4, axis=0)[:, :, half:].reshape(1, -1)
+    found_b = score(here, wanted_b, token_b, vocab_all)
+    triple = score(here, wanted_a, (token_a,), vocab_all, found_b)
     triples = exchange(triple, ("z", "x"))
     triples = triples.reshape(BLOCKS, half, 128)[:, :, :6].reshape(BLOCKS, half, 2, 3)
     tops, totals, picks = triples[..., 0], triples[..., 1], triples[..., 2]

time: 192 us -> 188 us (0.979)
  blocking collectives: 61.1 us -> 44.6 us
  waiting for transfers between devices: 55.8 us -> 64.1 us
  starting transfers between devices: 21 us -> 24.2 us
    all_to_all x5 -> x4, blocking collectives: 61.1 us -> 44.6 us  [exchange(): return lax.all_to_all(value, axes, split_axis=0, concat_axis=0, tiled=True)]
    ppermute x0 -> x4, waiting for transfers between devices: none -> 13.6 us  [the longest x1 9.26 us: inner(): one_up = lax.ppermute(far_b, 'x', up)]
    all_to_all x3, waiting for transfers between devices: 55.1 us -> 49.7 us  [exchange(): return lax.all_to_all(value, axes, split_axis=0, concat_axis=0, tiled=True)]
    ppermute x0 -> x4, starting transfers between devices: none -> 4.39 us  [the longest x1 2.05 us: inner(): two_down = lax.ppermute(one_down[quarter:], 'x', down)]
  transfers between devices with their start and end apart: 5 -> 9, of which waited for: 3 -> 7; matrix products, arithmetic and copies ran while one was open for 9% -> 9% of each run, Pallas kernels for 6% -> 6%
where the time goes in v4:
time: 188 us; the launch traced here: 186 us
  waiting for transfers between devices  64.1 us (34%)
  blocking collectives  44.6 us (24%)
  starting transfers between devices  24.2 us (13%)
  Pallas kernels  21.4 us (11%)
  between operations  14.5 us (8%)
  matrix products  8.05 us (4%)
  other arithmetic  5.64 us (3%)
  local copies, waits for them, and re-layouts  3.7 us (2%)
    all_to_all x3, waiting for transfers between devices, exchange(): return lax.all_to_all(value, axes, split_axis=0, concat_axis=0, tiled=True)  49.7 us
    all_to_all x4, blocking collectives, exchange(): return lax.all_to_all(value, axes, split_axis=0, concat_axis=0, tiled=True)  44.6 us
    all_to_all x3, starting transfers between devices, exchange(): return lax.all_to_all(value, axes, split_axis=0, concat_axis=0, tiled=True)  19.7 us
    pallas_call x2, Pallas kernels, score(): pl.pallas_call(functools.partial(score_kernel, count=count, parts=len(tok...  18.7 us
    ppermute x1, waiting for transfers between devices, inner(): one_up = lax.ppermute(far_b, 'x', up)  9.26 us
    dot_general x1, matrix products, inner(): partial = jnp.dot(normed_inner, w_out, preferred_element_type=jnp.float32)  4.99 us
    ppermute x1, waiting for transfers between devices, inner(): two_up = lax.ppermute(one_up[:quarter], 'x', up)  3.77 us
  transfers between devices with their start and end apart: 9, of which 7 were waited for; matrix products, arithmetic and copies ran while one was open for 9% of the time, Pallas kernels for 6%

profile of v4, /device:TPU:2, one launch (start us, length us, event | category | flops | bytes accessed | tf_op | source)
XLA Modules:
  0.0 186.1 jit_solution(12615657982574151410)
XLA Ops:
  7.2 0.0 copy-start
  7.2 0.0 all-gather.3.cloned.1.call-start
  7.3 0.7 all-gather.3.cloned.1.call-update
  8.0 0.1 copy.40
  8.1 0.1 copy.46
  8.2 0.2 reduce_window_sum.11
  8.4 0.1 copy.47
  8.5 0.2 copy.43
  8.7 0.0 copy-start.3
  8.7 0.0 copy-start.11
  8.8 0.6 fusion.1
  9.4 1.0 pad_maximum_fusion
  10.4 11.5 %all-to-all-start = ((f16[32,8,1152]{2,1,0:T(8,128)(2,1)}), f16[32,8,1152]{2,1,0:T(8,128)(2,1)S(1)}, u32[]{:S(2)}, u32[]{:S(2)}) async-start(f16[32,8,1152]{2,1,0:T(8,128)(2,1)} %pad_maximum_fusion), calls=%async_computation | async-start | bytes 1179648 | tf_op jit(solution)/shard_map/all_to_all | solution.py:150
  21.9 0.1 copy.45
  21.9 0.1 copy.41
  22.0 0.2 copy.48
  22.2 0.1 broadcast_in_dim.32
  22.3 0.1 mul.127
  22.4 0.1 copy.50
  22.4 18.5 %all-to-all-done = f16[32,8,1152]{2,1,0:T(8,128)(2,1)S(1)} async-done(((f16[32,8,1152]{2,1,0:T(8,128)(2,1)}), f16[32,8,1152]{2,1,0:T(8,128)(2,1)S(1)}, u32[]{:S(2)}, u32[]{:S(2)}) %all-to-all-start) | async-done | bytes 589856 | tf_op jit(solution)/shard_map/all_to_all | solution.py:150
  41.0 1.1 bitcast_convert_fusion.recv_ref
  42.1 2.7 %scan_states.1 = f32[256,1024]{1,0:T(8,128)} custom-call(f32[256,1152]{1,0:T(8,128)} %bitcast_convert_fusion.recv_ref), custom_call_target="tpu_custom_call" | custom-call | tf_op jit(solution)/shard_map/scan_states/pallas_call | solution.py:53
  44.8 2.1 %convert_bitcast_fusion = f16[32,8,1024]{2,1,0:T(8,128)(2,1)} fusion(f32[256,1024]{1,0:T(8,128)} %scan_states.1), kind=kLoop, calls=%fused_computation.34 | loop fusion | flops 262144 | bytes 1572864 | tf_op jit(solution)/shard_map/all_to_all | solution.py:150
  46.9 4.8 %all-to-all-start.1 = ((f16[32,8,1024]{2,1,0:T(8,128)(2,1)}), f16[32,8,1024]{2,1,0:T(8,128)(2,1)S(1)}, u32[]{:S(2)}, u32[]{:S(2)}) async-start(f16[32,8,1024]{2,1,0:T(8,128)(2,1)} %convert_bitcast_fusion), calls=%async_computation.1 | async-start | bytes 1048576 | tf_op jit(solution)/shard_map/all_to_all | solution.py:150
  51.6 0.0 all-gather.5.cloned.1.call-start
  51.8 0.1 fusion.53
  51.9 1.4 fusion.7
  53.3 15.2 %all-to-all-done.1 = f16[32,8,1024]{2,1,0:T(8,128)(2,1)S(1)} async-done(((f16[32,8,1024]{2,1,0:T(8,128)(2,1)}), f16[32,8,1024]{2,1,0:T(8,128)(2,1)S(1)}, u32[]{:S(2)}, u32[]{:S(2)}) %all-to-all-start.1) | async-done | bytes 524320 | tf_op jit(solution)/shard_map/all_to_all | solution.py:150
  68.6 0.9 multiply_reduce_fusion
  69.5 5.0 %fusion = f16[128,4096]{1,0:T(8,128)(2,1)S(1)} fusion(bf16[1024,4096]{1,0:T(8,128)(2,1)} %param.21, f32[128,1024]{0,1:T(8,128)S(1)} %get-tuple-element.17, f32[1024]{0:T(1024)S(1)} %copy-done.5, f32[128]{0:T(128)S(1)} %add_rsqrt_fusion.1), kind=kOutput, calls=%fused_computation.2 | convolution fusion | flops 1075183616 | bytes 9966080 | tf_op jit(solution)/shard_map/dot_general | solution.py:206
  74.5 0.2 copy.49
  74.7 4.6 %all_to_all.59 = f16[2,64,4096]{2,1,0:T(8,128)(2,1)S(1)} all-to-all(f16[2,64,4096]{2,1,0:T(8,128)(2,1)S(1)} %bitcast.74), channel_id=1, replica_groups=mesh['z'=8,'y'=4,'x'=4,'core'=2] {'core'}, dimensions={0} | all-to-all | bytes 2097152 | tf_op jit(solution)/shard_map/all_to_all | solution.py:150
  79.3 0.1 convert_element_type.83
  79.4 0.1 fusion.6
  79.6 0.1 pad_maximum_fusion.1
  79.7 0.0 copy-start.7
  79.7 13.2 %all_to_all.60 = f16[4,16,4224]{2,1,0:T(8,128)(2,1)S(1)} all-to-all(f16[4,16,4224]{2,1,0:T(8,128)(2,1)S(1)} %pad_maximum_fusion.1), channel_id=1, replica_groups=mesh['z'=8,'y'=4,'x'=4,'core'=2] {'x'}, dimensions={0} | all-to-all | bytes 1081344 | tf_op jit(solution)/shard_map/all_to_all | solution.py:150
  93.0 0.1 convert_element_type.86
  93.1 0.2 multiply_reduce_fusion.1
  93.3 0.1 multiply_convert_fusion.2
  93.5 9.7 %all_to_all.61 = bf16[4,8,4096]{2,1,0:T(8,128)(2,1)} all-to-all(bf16[4,8,4096]{2,1,0:T(8,128)(2,1)S(1)} %broadcast_in_dim.37), channel_id=1, replica_groups=mesh['z'=8,'y'=4,'x'=4,'core'=2] {'x'}, dimensions={0} | all-to-all | bytes 524288 | tf_op jit(solution)/shard_map/all_to_all | solution.py:150
  103.2 0.0 all-gather.5.cloned.1.call-update
  103.2 0.8 broadcast_in_dim.40
  104.1 3.5 %all-to-all-start.5 = ((bf16[8,8,4096]{2,1,0:T(8,128)(2,1)}), bf16[8,8,4096]{2,1,0:T(8,128)(2,1)S(1)}, u32[]{:S(2)}, u32[]{:S(2)}) async-start(bf16[8,8,4096]{2,1,0:T(8,128)(2,1)} %broadcast_in_dim.40), calls=%async_computation.5 | async-start | bytes 1048576 | tf_op jit(solution)/shard_map/all_to_all | solution.py:150
  107.6 16.0 %all-to-all-done.5 = bf16[8,8,4096]{2,1,0:T(8,128)(2,1)S(1)} async-done(((bf16[8,8,4096]{2,1,0:T(8,128)(2,1)}), bf16[8,8,4096]{2,1,0:T(8,128)(2,1)S(1)}, u32[]{:S(2)}, u32[]{:S(2)}) %all-to-all-start.5) | async-done | bytes 524320 | tf_op jit(solution)/shard_map/all_to_all | solution.py:150
  123.5 0.2 collective-permute-start
  123.8 1.8 collective-permute-start.2
  125.6 0.6 gather_fusion
  126.2 9.3 %collective-permute-done.refs_4_ = bf16[64,4096]{1,0:T(8,128)(2,1)S(1)} collective-permute-done((bf16[64,4096]{1,0:T(8,128)(2,1)S(1)}, bf16[64,4096]{1,0:T(8,128)(2,1)S(1)}, u32[]{:S(2)}, u32[]{:S(2)}) %collective-permute-start) | collective-permute-done | bytes 524320 | tf_op jit(solution)/shard_map/ppermute | solution.py:235
  135.5 0.3 collective-permute-start.1
  135.8 2.0 %collective-permute-start.3 = (bf16[32,4096]{1,0:T(8,128)(2,1)S(1)}, bf16[32,4096]{1,0:T(8,128)(2,1)S(1)}, u32[]{:S(2)}, u32[]{:S(2)}) collective-permute-start(bf16[32,4096]{1,0:T(8,128)(2,1)S(1)} %slice.82), channel_id=1, source_target_pairs={{0,6},{2,0},{4,2},{6,4},{1,7},{3,1},{5,3},{7,5},{8,14},{10,8},{12,... | collective-permute-start | bytes 786440 | tf_op jit(solution)/shard_map/ppermute | solution.py:238
  137.9 0.1 slice_select_fusion
  137.9 0.1 reshape.194.refs_1_
  138.0 0.1 reshape.193.refs_1_
  138.1 3.8 %collective-permute-done.1.refs_5_ = bf16[32,4096]{1,0:T(8,128)(2,1)S(1)} collective-permute-done((bf16[32,4096]{1,0:T(8,128)(2,1)S(1)}, bf16[32,4096]{1,0:T(8,128)(2,1)S(1)}, u32[]{:S(2)}, u32[]{:S(2)}) %collective-permute-start.1) | collective-permute-done | bytes 262176 | tf_op jit(solution)/shard_map/ppermute | solution.py:237
  141.9 0.5 collective-permute-done.3.refs_6_
  142.4 9.1 %score.2.refs_4_ = f32[256,128]{1,0:T(8,128)S(1)} custom-call(s32[1]{0:T(128)} %bitcast.20.refs_0_, s32[1,256]{1,0:T(1,128)S(1)} %reshape.194.refs_1_, bf16[2048,4096]{1,0:T(8,128)(2,1)} %all-gather.3.cloned.1.call-done.refs_2_, bf16[64,4096]{1,0:T(8,128)(2,1)S(1)} %bitcast.71, bf16[64,4096]{1,0:T(8,128)(2,1)S(1)} %collective-permute-done.refs_4_, ...), custom_call_target="tpu_custom_call" | custom-call | flops 4294967296 | bytes 18874368 | tf_op jit(solution)/shard_map/score/pallas_call | solution.py:122
  151.6 0.1 all-gather.5.cloned.1.call-done.refs_3_
  151.7 9.6 %score.3 = f32[256,128]{1,0:T(8,128)S(1)} custom-call(s32[1]{0:T(128)} %bitcast.20.refs_0_, s32[1,256]{1,0:T(1,128)S(1)} %reshape.193.refs_1_, bf16[2048,4096]{1,0:T(8,128)(2,1)} %all-gather.3.cloned.1.call-done.refs_2_, bf16[256,4096]{1,0:T(8,128)(2,1)} %all-gather.5.cloned.1.call-done.refs_3_, f32[256,128]{1,0:T(8,128)S(1)} %score.2.refs_4_), custom_call_target="tpu_custom_call" | custom-call | flops 4294967296 | bytes 18874368 | tf_op jit(solution)/shard_map/score/pallas_call | solution.py:122
  161.2 17.0 %all_to_all.62 = f32[32,8,128]{2,1,0:T(8,128)S(1)} all-to-all(f32[32,8,128]{2,1,0:T(8,128)S(1)} %bitcast.72), channel_id=1, replica_groups=mesh['z'=8,'y'=4,'x'=4,'core'=2] {'z','x'}, dimensions={0} | all-to-all | bytes 262144 | tf_op jit(solution)/shard_map/all_to_all | solution.py:150
  178.3 0.1 copy.53
  178.4 0.1 slice_reduce_fusion.1
  178.5 0.2 fusion.29
  178.7 0.6 reshape.196
  (48 shorter events, 0.5 us)
Async XLA Ops:
  7.2 1.6 copy-start
  7.2 0.8 copy-start.8
  7.2 0.9 copy-start.10
  7.2 1.2 copy-start.2
  7.2 135.2 %all-gather.3.cloned.1.call-start = ((), (), s32[]{:S(2)}) async-start(), calls=%async_computation.7 | async-start | bytes 18874368 | tf_op jit(solution)/shard_map/all_gather | solution.py:170
  8.7 13.3 %copy-start.3 = (bf16[128,1024]{1,0:T(8,128)(2,1)S(1)}, bf16[128,1024]{1,0:T(8,128)(2,1)}, u32[]{:S(2)}) copy-start(bf16[128,1024]{1,0:T(8,128)(2,1)} %param.14) | copy-start | bytes 786436
  8.7 13.5 %copy-start.11 = (f32[16]{0:T(128)S(1)}, f32[16]{0:T(128)}, u32[]{:S(2)}) copy-start(f32[16]{0:T(128)} %param.19) | copy-start | bytes 196
  8.7 13.6 %copy-start.9 = (s32[32,16]{0,1:T(8,128)S(1)}, s32[32,16]{0,1:T(8,128)}, u32[]{:S(2)}) copy-start(s32[32,16]{0,1:T(8,128)} %param.25) | copy-start | bytes 6148
  10.4 30.6 %all-to-all-start = ((f16[32,8,1152]{2,1,0:T(8,128)(2,1)}), f16[32,8,1152]{2,1,0:T(8,128)(2,1)S(1)}, u32[]{:S(2)}, u32[]{:S(2)}) async-start(f16[32,8,1152]{2,1,0:T(8,128)(2,1)} %pad_maximum_fusion), calls=%async_computation | async-start | bytes 1179648 | tf_op jit(solution)/shard_map/all_to_all | solution.py:150
  42.1 9.7 %copy-start.6 = (bf16[128,256]{1,0:T(8,128)(2,1)S(1)}, bf16[128,256]{1,0:T(8,128)(2,1)}, u32[]{:S(2)}) copy-start(bf16[128,256]{1,0:T(8,128)(2,1)} %param.16) | copy-start | bytes 196612
  46.9 21.7 %all-to-all-start.1 = ((f16[32,8,1024]{2,1,0:T(8,128)(2,1)}), f16[32,8,1024]{2,1,0:T(8,128)(2,1)S(1)}, u32[]{:S(2)}, u32[]{:S(2)}) async-start(f16[32,8,1024]{2,1,0:T(8,128)(2,1)} %convert_bitcast_fusion), calls=%async_computation.1 | async-start | bytes 1048576 | tf_op jit(solution)/shard_map/all_to_all | solution.py:150
  51.6 100.0 %all-gather.5.cloned.1.call-start = ((), (), s32[]{:S(2)}) async-start(), calls=%async_computation.8 | async-start | bytes 2359296 | tf_op jit(solution)/shard_map/all_gather | solution.py:230
  53.3 16.2 %copy-start.5 = (f32[1024]{0:T(1024)S(1)}, f32[1024]{0:T(1024)}, u32[]{:S(2)}) copy-start(f32[1024]{0:T(1024)} %param.20) | copy-start | bytes 12292
  79.7 13.4 %copy-start.4 = (bf16[16,4096]{1,0:T(8,128)(2,1)S(1)}, bf16[16,4096]{1,0:T(8,128)(2,1)}, u32[]{:S(2)}) copy-start(bf16[16,4096]{1,0:T(8,128)(2,1)} %param.22) | copy-start | bytes 393220
  79.7 13.6 %copy-start.7 = (f32[4096]{0:T(1024)S(1)}, f32[4096]{0:T(1024)}, u32[]{:S(2)}) copy-start(f32[4096]{0:T(1024)} %param.23) | copy-start | bytes 49156
  93.3 42.5 %copy-start.1 = (f32[16,4096]{1,0:T(8,128)}, f32[16,4096]{1,0:T(8,128)S(1)}, u32[]{:S(2)}) copy-start(f32[16,4096]{1,0:T(8,128)S(1)} %get-tuple-element.5) | copy-start | bytes 786436
  104.1 19.5 %all-to-all-start.5 = ((bf16[8,8,4096]{2,1,0:T(8,128)(2,1)}), bf16[8,8,4096]{2,1,0:T(8,128)(2,1)S(1)}, u32[]{:S(2)}, u32[]{:S(2)}) async-start(bf16[8,8,4096]{2,1,0:T(8,128)(2,1)} %broadcast_in_dim.40), calls=%async_computation.5 | async-start | bytes 1048576 | tf_op jit(solution)/shard_map/all_to_all | solution.py:150
  123.5 11.9 %collective-permute-start = (bf16[64,4096]{1,0:T(8,128)(2,1)S(1)}, bf16[64,4096]{1,0:T(8,128)(2,1)S(1)}, u32[]{:S(2)}, u32[]{:S(2)}) collective-permute-start(bf16[64,4096]{1,0:T(8,128)(2,1)S(1)} %bitcast.69), channel_id=1, source_target_pairs={{0,2},{2,4},{4,6},{6,0},{1,3},{3,5},{5,7},{7,1},{8,10},{10,12},{12... | collective-permute-start | bytes 1572872 | tf_op jit(solution)/shard_map/ppermute | solution.py:235
  123.8 12.0 %collective-permute-start.2 = (bf16[64,4096]{1,0:T(8,128)(2,1)S(1)}, bf16[64,4096]{1,0:T(8,128)(2,1)S(1)}, u32[]{:S(2)}, u32[]{:S(2)}) collective-permute-start(bf16[64,4096]{1,0:T(8,128)(2,1)S(1)} %bitcast.70), channel_id=1, source_target_pairs={{0,6},{2,0},{4,2},{6,4},{1,7},{3,1},{5,3},{7,5},{8,14},{10,8},{12,... | collective-permute-start | bytes 1572872 | tf_op jit(solution)/shard_map/ppermute | solution.py:236
  135.5 6.4 %collective-permute-start.1 = (bf16[32,4096]{1,0:T(8,128)(2,1)S(1)}, bf16[32,4096]{1,0:T(8,128)(2,1)S(1)}, u32[]{:S(2)}, u32[]{:S(2)}) collective-permute-start(bf16[32,4096]{1,0:T(8,128)(2,1)S(1)} %slice.81), channel_id=1, source_target_pairs={{0,2},{2,4},{4,6},{6,0},{1,3},{3,5},{5,7},{7,1},{8,10},{10,12},{12... | collective-permute-start | bytes 786440 | tf_op jit(solution)/shard_map/ppermute | solution.py:237
  135.8 6.6 %collective-permute-start.3 = (bf16[32,4096]{1,0:T(8,128)(2,1)S(1)}, bf16[32,4096]{1,0:T(8,128)(2,1)S(1)}, u32[]{:S(2)}, u32[]{:S(2)}) collective-permute-start(bf16[32,4096]{1,0:T(8,128)(2,1)S(1)} %slice.82), channel_id=1, source_target_pairs={{0,6},{2,0},{4,2},{6,4},{1,7},{3,1},{5,3},{7,5},{8,14},{10,8},{12,... | collective-permute-start | bytes 786440 | tf_op jit(solution)/shard_map/ppermute | solution.py:238
Sparse Core Ops, SparseCore 0:
  9.9 100.2 all-gather.2
  111.9 39.6 all-gather.4

commit v5 on v4

--- a/solution.py
+++ b/solution.py
@@ -226,11 +226,17 @@
     ).astype(jnp.bfloat16)
 
     half = rows // 2
-    near_a = exchange(copies(normed[:half], 4), "x")
+    here = lax.axis_index("x")
+    up = [(i, (i + 1) % 4) for i in range(4)]
+    across = [(i, (i + 2) % 4) for i in range(4)]
+    down = [(i, (i - 1) % 4) for i in range(4)]
+    first = normed[:half]
+    near_a = jnp.stack(
+        [first] + [lax.ppermute(first, "x", way) for way in (up, across, down)]
+    )
+    near_a = jnp.take(near_a, (here - jnp.arange(4)) % 4, axis=0).reshape(4 * half, -1)
     token_a = lax.all_gather(near_a, "z", axis=0, tiled=True)
     far_b = exchange(copies(normed[half:], 8), "z")
-    up = [(i, (i + 1) % 4) for i in range(4)]
-    down = [(i, (i - 1) % 4) for i in range(4)]
     quarter = far_b.shape[0] // 2
     one_up = lax.ppermute(far_b, "x", up)
     one_down = lax.ppermute(far_b, "x", down)
@@ -240,7 +246,6 @@
 
     ids = ids - (lax.axis_index("z") * (4 * SPAN) + lax.axis_index("x") * TILE)
     wanted_a = ids[:, :, :half].transpose(1, 0, 2).reshape(1, -1)
-    here = lax.axis_index("x")
     wanted_b = jnp.take(ids, (here - jnp.arange(4)) % 4, axis=0)[:, :, half:].reshape(1, -1)
     found_b = score(here, wanted_b, token_b, vocab_all)
     triple = score(here, wanted_a, (token_a,), vocab_all, found_b)

time: 188 us -> 187 us (level)
  starting transfers between devices: 24.2 us -> 29.8 us
  blocking collectives: 44.6 us -> 39.5 us
  waiting for transfers between devices: 64.1 us -> 61 us
    all_to_all x3, waiting for transfers between devices: 49.7 us -> 42.1 us  [exchange(): return lax.all_to_all(value, axes, split_axis=0, concat_axis=0, tiled=True)]
    all_to_all x4 -> x3, blocking collectives: 44.6 us -> 39.5 us  [exchange(): return lax.all_to_all(value, axes, split_axis=0, concat_axis=0, tiled=True)]
    ppermute x0 -> x3, starting transfers between devices: none -> 4.16 us  [inner(): lax.ppermute(first, 'x', way)]
    ppermute x0 -> x3, waiting for transfers between devices: none -> 3.7 us  [inner(): lax.ppermute(first, 'x', way)]
  transfers between devices with their start and end apart: 9 -> 12, of which waited for: 7 -> 10; matrix products, arithmetic and copies ran while one was open for 9% -> 10% of each run, Pallas kernels for 6% -> 6%
where the time goes in v5:
time: 187 us; the launch traced here: 185 us
  waiting for transfers between devices  61 us (33%)
  blocking collectives  39.5 us (21%)
  starting transfers between devices  29.8 us (16%)
  Pallas kernels  21.4 us (11%)
  between operations  14.4 us (8%)
  matrix products  8.04 us (4%)
  other arithmetic  7.31 us (4%)
  local copies, waits for them, and re-layouts  3.61 us (2%)
    all_to_all x3, waiting for transfers between devices, exchange(): return lax.all_to_all(value, axes, split_axis=0, concat_axis=0, tiled=True)  42.1 us
    all_to_all x3, blocking collectives, exchange(): return lax.all_to_all(value, axes, split_axis=0, concat_axis=0, tiled=True)  39.5 us
    all_to_all x3, starting transfers between devices, exchange(): return lax.all_to_all(value, axes, split_axis=0, concat_axis=0, tiled=True)  21.2 us
    pallas_call x2, Pallas kernels, score(): pl.pallas_call(functools.partial(score_kernel, count=count, parts=len(tok...  18.7 us
    ppermute x1, waiting for transfers between devices, inner(): one_up = lax.ppermute(far_b, 'x', up)  9.11 us
    dot_general x1, matrix products, inner(): partial = jnp.dot(normed_inner, w_out, preferred_element_type=jnp.float32)  4.97 us
    ppermute x3, starting transfers between devices, inner(): lax.ppermute(first, 'x', way)  4.16 us
    ppermute x1, waiting for transfers between devices, inner(): two_up = lax.ppermute(one_up[:quarter], 'x', up)  3.96 us
  transfers between devices with their start and end apart: 12, of which 10 were waited for; matrix products, arithmetic and copies ran while one was open for 10% of the time, Pallas kernels for 6%

profile of v5, /device:TPU:2, one launch (start us, length us, event | category | flops | bytes accessed | tf_op | source)
XLA Modules:
  0.0 185.0 jit_solution(8517985578790229976)
XLA Ops:
  7.3 0.7 all-gather.3.cloned.1.call-update
  8.0 0.1 copy.40
  8.1 0.1 copy.46
  8.2 0.2 reduce_window_sum.11
  8.4 0.1 copy.47
  8.5 0.2 copy.43
  8.8 0.6 fusion.1
  9.4 1.0 pad_maximum_fusion
  10.4 11.5 %all-to-all-start = ((f16[32,8,1152]{2,1,0:T(8,128)(2,1)}), f16[32,8,1152]{2,1,0:T(8,128)(2,1)S(1)}, u32[]{:S(2)}, u32[]{:S(2)}) async-start(f16[32,8,1152]{2,1,0:T(8,128)(2,1)} %pad_maximum_fusion), calls=%async_computation | async-start | bytes 1179648 | tf_op jit(solution)/shard_map/all_to_all | solution.py:150
  21.9 0.1 copy.41
  22.0 0.2 copy.48
  22.2 0.1 broadcast_in_dim.74
  22.3 0.1 mul.127
  22.4 0.1 copy.50
  22.4 18.5 %all-to-all-done = f16[32,8,1152]{2,1,0:T(8,128)(2,1)S(1)} async-done(((f16[32,8,1152]{2,1,0:T(8,128)(2,1)}), f16[32,8,1152]{2,1,0:T(8,128)(2,1)S(1)}, u32[]{:S(2)}, u32[]{:S(2)}) %all-to-all-start) | async-done | bytes 589856 | tf_op jit(solution)/shard_map/all_to_all | solution.py:150
  41.0 1.1 bitcast_convert_fusion.recv_ref
  42.1 2.7 %scan_states.1 = f32[256,1024]{1,0:T(8,128)} custom-call(f32[256,1152]{1,0:T(8,128)} %bitcast_convert_fusion.recv_ref), custom_call_target="tpu_custom_call" | custom-call | tf_op jit(solution)/shard_map/scan_states/pallas_call | solution.py:53
  44.8 2.1 %convert_bitcast_fusion = f16[32,8,1024]{2,1,0:T(8,128)(2,1)} fusion(f32[256,1024]{1,0:T(8,128)} %scan_states.1), kind=kLoop, calls=%fused_computation.35 | loop fusion | flops 262144 | bytes 1572864 | tf_op jit(solution)/shard_map/all_to_all | solution.py:150
  46.9 4.8 %all-to-all-start.1 = ((f16[32,8,1024]{2,1,0:T(8,128)(2,1)}), f16[32,8,1024]{2,1,0:T(8,128)(2,1)S(1)}, u32[]{:S(2)}, u32[]{:S(2)}) async-start(f16[32,8,1024]{2,1,0:T(8,128)(2,1)} %convert_bitcast_fusion), calls=%async_computation.1 | async-start | bytes 1048576 | tf_op jit(solution)/shard_map/all_to_all | solution.py:150
  51.7 0.1 fusion.53
  51.9 1.4 fusion.7
  53.3 15.3 %all-to-all-done.1 = f16[32,8,1024]{2,1,0:T(8,128)(2,1)S(1)} async-done(((f16[32,8,1024]{2,1,0:T(8,128)(2,1)}), f16[32,8,1024]{2,1,0:T(8,128)(2,1)S(1)}, u32[]{:S(2)}, u32[]{:S(2)}) %all-to-all-start.1) | async-done | bytes 524320 | tf_op jit(solution)/shard_map/all_to_all | solution.py:150
  68.6 0.9 multiply_reduce_fusion
  69.5 5.0 %fusion = f16[128,4096]{1,0:T(8,128)(2,1)S(1)} fusion(bf16[1024,4096]{1,0:T(8,128)(2,1)} %param.21, f32[128,1024]{0,1:T(8,128)S(1)} %get-tuple-element.18, f32[1024]{0:T(1024)S(1)} %copy-done.5, f32[128]{0:T(128)S(1)} %add_rsqrt_fusion.1), kind=kOutput, calls=%fused_computation.3 | convolution fusion | flops 1075183616 | bytes 9966080 | tf_op jit(solution)/shard_map/dot_general | solution.py:206
  74.5 0.2 copy.49
  74.7 4.6 %all_to_all.50 = f16[2,64,4096]{2,1,0:T(8,128)(2,1)S(1)} all-to-all(f16[2,64,4096]{2,1,0:T(8,128)(2,1)S(1)} %bitcast.80), channel_id=1, replica_groups=mesh['z'=8,'y'=4,'x'=4,'core'=2] {'core'}, dimensions={0} | all-to-all | bytes 2097152 | tf_op jit(solution)/shard_map/all_to_all | solution.py:150
  79.3 0.1 convert_element_type.83
  79.4 0.1 fusion.6
  79.6 0.9 pad_maximum_fusion.1
  80.5 5.0 %all-to-all-start.3 = ((f16[4,16,4224]{2,1,0:T(8,128)(2,1)}), f16[4,16,4224]{2,1,0:T(8,128)(2,1)S(1)}, u32[]{:S(2)}, u32[]{:S(2)}) async-start(f16[4,16,4224]{2,1,0:T(8,128)(2,1)} %pad_maximum_fusion.1), calls=%async_computation.3 | async-start | bytes 1081344 | tf_op jit(solution)/shard_map/all_to_all | solution.py:150
  85.5 0.1 broadcast_in_dim.79
  85.6 0.1 broadcast_in_dim.80
  85.7 8.3 %all-to-all-done.3 = f16[4,16,4224]{2,1,0:T(8,128)(2,1)S(1)} async-done(((f16[4,16,4224]{2,1,0:T(8,128)(2,1)}), f16[4,16,4224]{2,1,0:T(8,128)(2,1)S(1)}, u32[]{:S(2)}, u32[]{:S(2)}) %all-to-all-start.3) | async-done | bytes 540704 | tf_op jit(solution)/shard_map/all_to_all | solution.py:150
  94.0 0.1 convert_element_type.86
  94.1 0.2 multiply_reduce_fusion.1
  94.3 0.1 multiply_convert_fusion.2
  94.4 0.1 collective-permute-start
  94.5 3.5 %collective-permute-start.1 = (bf16[8,4096]{1,0:T(8,128)(2,1)S(1)}, bf16[8,4096]{1,0:T(8,128)(2,1)S(1)}, u32[]{:S(2)}, u32[]{:S(2)}) collective-permute-start(bf16[8,4096]{1,0:T(8,128)(2,1)S(1)} %get-tuple-element.8), channel_id=1, source_target_pairs={{0,4},{2,6},{4,0},{6,2},{1,5},{3,7},{5,1},{7,3},{8,12},{10,14},{12... | collective-permute-start | bytes 196616 | tf_op jit(solution)/shard_map/ppermute | solution.py:235
  98.1 0.6 collective-permute-start.2
  98.6 0.7 collective-permute-done
  99.3 1.2 collective-permute-done.1
  100.5 1.8 collective-permute-done.2
  102.4 0.6 gather_fusion
  102.9 0.8 bitcast_select_fusion
  103.8 19.0 %all_to_all.51 = bf16[8,8,4096]{2,1,0:T(8,128)(2,1)S(1)} all-to-all(bf16[8,8,4096]{2,1,0:T(8,128)(2,1)S(1)} %broadcast_in_dim.85), channel_id=1, replica_groups=mesh['z'=8,'y'=4,'x'=4,'core'=2] {'z'}, dimensions={0} | all-to-all | bytes 1048576 | tf_op jit(solution)/shard_map/all_to_all | solution.py:150
  122.8 0.2 collective-permute-start.3
  123.0 1.8 collective-permute-start.5
  124.8 0.6 gather_fusion.1
  125.4 9.1 %collective-permute-done.3.refs_4_ = bf16[64,4096]{1,0:T(8,128)(2,1)S(1)} collective-permute-done((bf16[64,4096]{1,0:T(8,128)(2,1)S(1)}, bf16[64,4096]{1,0:T(8,128)(2,1)S(1)}, u32[]{:S(2)}, u32[]{:S(2)}) %collective-permute-start.3) | collective-permute-done | bytes 524320 | tf_op jit(solution)/shard_map/ppermute | solution.py:241
  134.5 0.5 collective-permute-start.4
  135.0 1.9 %collective-permute-start.6 = (bf16[32,4096]{1,0:T(8,128)(2,1)S(1)}, bf16[32,4096]{1,0:T(8,128)(2,1)S(1)}, u32[]{:S(2)}, u32[]{:S(2)}) collective-permute-start(bf16[32,4096]{1,0:T(8,128)(2,1)S(1)} %slice.84), channel_id=1, source_target_pairs={{0,6},{2,0},{4,2},{6,4},{1,7},{3,1},{5,3},{7,5},{8,14},{10,8},{12,... | collective-permute-start | bytes 786440 | tf_op jit(solution)/shard_map/ppermute | solution.py:244
  136.9 0.1 slice_select_fusion
  137.0 0.1 reshape.192.refs_1_
  137.1 0.1 reshape.191.refs_1_
  137.2 4.0 %collective-permute-done.4.refs_5_ = bf16[32,4096]{1,0:T(8,128)(2,1)S(1)} collective-permute-done((bf16[32,4096]{1,0:T(8,128)(2,1)S(1)}, bf16[32,4096]{1,0:T(8,128)(2,1)S(1)}, u32[]{:S(2)}, u32[]{:S(2)}) %collective-permute-start.4) | collective-permute-done | bytes 262176 | tf_op jit(solution)/shard_map/ppermute | solution.py:243
  141.2 0.4 collective-permute-done.6.refs_6_
  141.6 9.1 %score.2.refs_4_ = f32[256,128]{1,0:T(8,128)S(1)} custom-call(s32[1]{0:T(128)} %bitcast.20.refs_0_, s32[1,256]{1,0:T(1,128)S(1)} %reshape.192.refs_1_, bf16[2048,4096]{1,0:T(8,128)(2,1)} %all-gather.3.cloned.1.call-done.refs_2_, bf16[64,4096]{1,0:T(8,128)(2,1)S(1)} %bitcast.77, bf16[64,4096]{1,0:T(8,128)(2,1)S(1)} %collective-permute-done.3.refs_4_, ...), custom_call_target="tpu_custom_call" | custom-call | flops 4294967296 | bytes 18874368 | tf_op jit(solution)/shard_map/score/pallas_call | solution.py:122
  150.7 1.0 all-gather.5.cloned.1.call-done.refs_3_
  151.7 9.6 %score.3 = f32[256,128]{1,0:T(8,128)S(1)} custom-call(s32[1]{0:T(128)} %bitcast.20.refs_0_, s32[1,256]{1,0:T(1,128)S(1)} %reshape.191.refs_1_, bf16[2048,4096]{1,0:T(8,128)(2,1)} %all-gather.3.cloned.1.call-done.refs_2_, bf16[256,4096]{1,0:T(8,128)(2,1)} %all-gather.5.cloned.1.call-done.refs_3_, f32[256,128]{1,0:T(8,128)S(1)} %score.2.refs_4_), custom_call_target="tpu_custom_call" | custom-call | flops 4294967296 | bytes 18874368 | tf_op jit(solution)/shard_map/score/pallas_call | solution.py:122
  161.2 15.9 %all_to_all.52 = f32[32,8,128]{2,1,0:T(8,128)S(1)} all-to-all(f32[32,8,128]{2,1,0:T(8,128)S(1)} %bitcast.78), channel_id=1, replica_groups=mesh['z'=8,'y'=4,'x'=4,'core'=2] {'z','x'}, dimensions={0} | all-to-all | bytes 262144 | tf_op jit(solution)/shard_map/all_to_all | solution.py:150
  177.2 0.1 copy.53
  177.3 0.1 slice_reduce_fusion.1
  177.4 0.2 fusion.29
  177.6 0.6 reshape.194
  (57 shorter events, 0.6 us)
Async XLA Ops:
  7.2 1.6 copy-start
  7.2 0.8 copy-start.8
  7.2 0.9 copy-start.10
  7.2 1.2 copy-start.2
  7.2 134.3 %all-gather.3.cloned.1.call-start = ((), (), s32[]{:S(2)}) async-start(), calls=%async_computation.6 | async-start | bytes 18874368 | tf_op jit(solution)/shard_map/all_gather | solution.py:170
  8.7 13.3 %copy-start.3 = (bf16[128,1024]{1,0:T(8,128)(2,1)S(1)}, bf16[128,1024]{1,0:T(8,128)(2,1)}, u32[]{:S(2)}) copy-start(bf16[128,1024]{1,0:T(8,128)(2,1)} %param.14) | copy-start | bytes 786436
  8.7 13.5 %copy-start.11 = (f32[16]{0:T(128)S(1)}, f32[16]{0:T(128)}, u32[]{:S(2)}) copy-start(f32[16]{0:T(128)} %param.19) | copy-start | bytes 196
  8.7 13.6 %copy-start.9 = (s32[32,16]{0,1:T(8,128)S(1)}, s32[32,16]{0,1:T(8,128)}, u32[]{:S(2)}) copy-start(s32[32,16]{0,1:T(8,128)} %param.25) | copy-start | bytes 6148
  10.4 30.6 %all-to-all-start = ((f16[32,8,1152]{2,1,0:T(8,128)(2,1)}), f16[32,8,1152]{2,1,0:T(8,128)(2,1)S(1)}, u32[]{:S(2)}, u32[]{:S(2)}) async-start(f16[32,8,1152]{2,1,0:T(8,128)(2,1)} %pad_maximum_fusion), calls=%async_computation | async-start | bytes 1179648 | tf_op jit(solution)/shard_map/all_to_all | solution.py:150
  42.1 9.6 %copy-start.6 = (bf16[128,256]{1,0:T(8,128)(2,1)S(1)}, bf16[128,256]{1,0:T(8,128)(2,1)}, u32[]{:S(2)}) copy-start(bf16[128,256]{1,0:T(8,128)(2,1)} %param.16) | copy-start | bytes 196612
  46.9 21.7 %all-to-all-start.1 = ((f16[32,8,1024]{2,1,0:T(8,128)(2,1)}), f16[32,8,1024]{2,1,0:T(8,128)(2,1)S(1)}, u32[]{:S(2)}, u32[]{:S(2)}) async-start(f16[32,8,1024]{2,1,0:T(8,128)(2,1)} %convert_bitcast_fusion), calls=%async_computation.1 | async-start | bytes 1048576 | tf_op jit(solution)/shard_map/all_to_all | solution.py:150
  53.3 16.2 %copy-start.5 = (f32[1024]{0:T(1024)S(1)}, f32[1024]{0:T(1024)}, u32[]{:S(2)}) copy-start(f32[1024]{0:T(1024)} %param.20) | copy-start | bytes 12292
  80.5 13.6 %copy-start.4 = (bf16[16,4096]{1,0:T(8,128)(2,1)S(1)}, bf16[16,4096]{1,0:T(8,128)(2,1)}, u32[]{:S(2)}) copy-start(bf16[16,4096]{1,0:T(8,128)(2,1)} %param.22) | copy-start | bytes 393220
  80.5 13.8 %copy-start.7 = (f32[4096]{0:T(1024)S(1)}, f32[4096]{0:T(1024)}, u32[]{:S(2)}) copy-start(f32[4096]{0:T(1024)} %param.23) | copy-start | bytes 49156
  80.5 13.5 %all-to-all-start.3 = ((f16[4,16,4224]{2,1,0:T(8,128)(2,1)}), f16[4,16,4224]{2,1,0:T(8,128)(2,1)S(1)}, u32[]{:S(2)}, u32[]{:S(2)}) async-start(f16[4,16,4224]{2,1,0:T(8,128)(2,1)} %pad_maximum_fusion.1), calls=%async_computation.3 | async-start | bytes 1081344 | tf_op jit(solution)/shard_map/all_to_all | solution.py:150
  85.5 66.2 %all-gather.5.cloned.1.call-start = ((), (), s32[]{:S(2)}) async-start(), calls=%async_computation.7 | async-start | bytes 2359296 | tf_op jit(solution)/shard_map/all_gather | solution.py:238
  94.3 28.5 %copy-start.1 = (f32[16,4096]{1,0:T(8,128)}, f32[16,4096]{1,0:T(8,128)S(1)}, u32[]{:S(2)}) copy-start(f32[16,4096]{1,0:T(8,128)S(1)} %get-tuple-element.5) | copy-start | bytes 786436
  94.4 4.9 %collective-permute-start = (bf16[8,4096]{1,0:T(8,128)(2,1)S(1)}, bf16[8,4096]{1,0:T(8,128)(2,1)S(1)}, u32[]{:S(2)}, u32[]{:S(2)}) collective-permute-start(bf16[8,4096]{1,0:T(8,128)(2,1)S(1)} %get-tuple-element.8), channel_id=1, source_target_pairs={{0,2},{2,4},{4,6},{6,0},{1,3},{3,5},{5,7},{7,1},{8,10},{10,12},{12... | collective-permute-start | bytes 196616 | tf_op jit(solution)/shard_map/ppermute | solution.py:235
  94.5 6.0 %collective-permute-start.1 = (bf16[8,4096]{1,0:T(8,128)(2,1)S(1)}, bf16[8,4096]{1,0:T(8,128)(2,1)S(1)}, u32[]{:S(2)}, u32[]{:S(2)}) collective-permute-start(bf16[8,4096]{1,0:T(8,128)(2,1)S(1)} %get-tuple-element.8), channel_id=1, source_target_pairs={{0,4},{2,6},{4,0},{6,2},{1,5},{3,7},{5,1},{7,3},{8,12},{10,14},{12... | collective-permute-start | bytes 196616 | tf_op jit(solution)/shard_map/ppermute | solution.py:235
  98.1 4.3 %collective-permute-start.2 = (bf16[8,4096]{1,0:T(8,128)(2,1)S(1)}, bf16[8,4096]{1,0:T(8,128)(2,1)S(1)}, u32[]{:S(2)}, u32[]{:S(2)}) collective-permute-start(bf16[8,4096]{1,0:T(8,128)(2,1)S(1)} %get-tuple-element.8), channel_id=1, source_target_pairs={{0,6},{2,0},{4,2},{6,4},{1,7},{3,1},{5,3},{7,5},{8,14},{10,8},{12,... | collective-permute-start | bytes 196616 | tf_op jit(solution)/shard_map/ppermute | solution.py:235
  122.8 11.7 %collective-permute-start.3 = (bf16[64,4096]{1,0:T(8,128)(2,1)S(1)}, bf16[64,4096]{1,0:T(8,128)(2,1)S(1)}, u32[]{:S(2)}, u32[]{:S(2)}) collective-permute-start(bf16[64,4096]{1,0:T(8,128)(2,1)S(1)} %bitcast.75), channel_id=1, source_target_pairs={{0,2},{2,4},{4,6},{6,0},{1,3},{3,5},{5,7},{7,1},{8,10},{10,12},{12... | collective-permute-start | bytes 1572872 | tf_op jit(solution)/shard_map/ppermute | solution.py:241
  123.0 12.0 %collective-permute-start.5 = (bf16[64,4096]{1,0:T(8,128)(2,1)S(1)}, bf16[64,4096]{1,0:T(8,128)(2,1)S(1)}, u32[]{:S(2)}, u32[]{:S(2)}) collective-permute-start(bf16[64,4096]{1,0:T(8,128)(2,1)S(1)} %bitcast.76), channel_id=1, source_target_pairs={{0,6},{2,0},{4,2},{6,4},{1,7},{3,1},{5,3},{7,5},{8,14},{10,8},{12,... | collective-permute-start | bytes 1572872 | tf_op jit(solution)/shard_map/ppermute | solution.py:242
  134.5 6.6 %collective-permute-start.4 = (bf16[32,4096]{1,0:T(8,128)(2,1)S(1)}, bf16[32,4096]{1,0:T(8,128)(2,1)S(1)}, u32[]{:S(2)}, u32[]{:S(2)}) collective-permute-start(bf16[32,4096]{1,0:T(8,128)(2,1)S(1)} %slice.83), channel_id=1, source_target_pairs={{0,2},{2,4},{4,6},{6,0},{1,3},{3,5},{5,7},{7,1},{8,10},{10,12},{12... | collective-permute-start | bytes 786440 | tf_op jit(solution)/shard_map/ppermute | solution.py:243
  135.0 6.5 %collective-permute-start.6 = (bf16[32,4096]{1,0:T(8,128)(2,1)S(1)}, bf16[32,4096]{1,0:T(8,128)(2,1)S(1)}, u32[]{:S(2)}, u32[]{:S(2)}) collective-permute-start(bf16[32,4096]{1,0:T(8,128)(2,1)S(1)} %slice.84), channel_id=1, source_target_pairs={{0,6},{2,0},{4,2},{6,4},{1,7},{3,1},{5,3},{7,5},{8,14},{10,8},{12,... | collective-permute-start | bytes 786440 | tf_op jit(solution)/shard_map/ppermute | solution.py:244
Sparse Core Ops, SparseCore 0:
  9.9 100.2 all-gather.2
  111.9 39.6 all-gather.4
